TPU v7x, 32 devices: a whole 2x2x4 slice. The times are simulated.
32 devices in a mesh: fsdp: 32 (over z, y, x, core).
Axes of the slice: x: 2, y: 2, z: 4, core: 2. Of those that a mesh axis runs over, the one named last changes fastest.
Arguments:
- inputs: bfloat16 [32, 128, 768], P('fsdp'), may hold values from -6 to 6
- encoded: bfloat16 [32, 64, 768], P('fsdp')
- lengths: int32 [32], P('fsdp'), may hold values from 32 to 128, as said below
- bucket_ids: int32 [128], replicated, may hold values from 0 to 31, as said below
- qkv_weights: bfloat16 [768, 6, 768], P('fsdp')
- out_weights: bfloat16 [768, 2, 768], P('fsdp'), may hold values from -1.75 to 1.75
- ff_in: bfloat16 [768, 2, 2048], P('fsdp'), may hold values from -0.21875 to 0.21875
- ff_out: bfloat16 [2048, 768], P('fsdp'), may hold values from -0.125 to 0.125
- gains: bfloat16 [3, 768], P(None, 'fsdp'), may hold values from 0.5 to 1.5
- bias_table: float32 [32, 12], replicated
- cotangent: bfloat16 [32, 128, 768], P('fsdp'), may hold values from -6 to 6
Outputs:
- outputs: bfloat16 [32, 128, 768], P('fsdp')
- input_grad: bfloat16 [32, 128, 768], P('fsdp')
- encoded_grad: bfloat16 [32, 64, 768], P('fsdp')
- qkv_grad: float32 [768, 6, 768], P('fsdp')
- out_grad: float32 [768, 2, 768], P('fsdp')
- ffin_grad: float32 [768, 2, 2048], P('fsdp')
- ffout_grad: float32 [2048, 768], P('fsdp')
- gain_grad: float32 [3, 768], P(None, 'fsdp')
- table_grad: float32 [32, 12], replicated
Inputs may be any that keep to these rules, and one draw needn't show every extreme that they name: `lengths`: some sequence uses all 128 slots. `bucket_ids`: non-decreasing in the distance; distance 0 has bucket 0 and distance 128 - 1 bucket 32 - 1.
All inputs are finite; a program needn't handle non-finite values.
Results may differ from a plain program's by a relative error of at most 0.02.
Values may be sent and summed in bfloat16 or wider, within the bound.
A program may use at most 192 MiB of HBM per device.

v0:
```python
import jax
import jax.numpy as jnp
from jax import lax
from jax.sharding import PartitionSpec as P

HEAD = 64


EPS = 1e-06


def prod(form, left, right):
    return jnp.einsum(form, left, right, preferred_element_type=jnp.float32)


def gelu_tanh(value):
    return (
        0.5
        * value
        * (1.0 + jnp.tanh(0.7978845608028654 * (value + 0.044715 * value * value * value)))
    )


def rms_fwd(value, gain):
    recip = lax.rsqrt(jnp.mean(value * value, axis=-1, keepdims=True) + EPS)
    normed = value * recip
    return ((normed * gain).astype(jnp.bfloat16), normed, recip)


def rms_bwd(grad, normed, recip, gain):
    scaled = grad * gain
    gain_grad = jnp.sum(grad * normed, axis=0)
    back = recip * (scaled - normed * jnp.mean(scaled * normed, axis=-1, keepdims=True))
    return (back, gain_grad)


def toeplitz_bias(bucket_ids, table, positions):
    onehot = (bucket_ids[:, None] == jnp.arange(table.shape[0], dtype=jnp.int32)[None, :]).astype(
        jnp.float32
    )
    by_dist = jnp.transpose(jnp.dot(onehot, table, precision=lax.Precision.HIGHEST), (1, 0))
    head_count = by_dist.shape[0]
    nearest = jnp.broadcast_to(by_dist[:, 0:1], (head_count, positions))
    cyclic = jnp.concatenate(
        [nearest, jnp.zeros((head_count, 1), jnp.float32), by_dist[:, :0:-1]], axis=1
    )
    tiled = jnp.broadcast_to(cyclic[:, None, :], (head_count, positions, 2 * positions))
    tiled = tiled.reshape(head_count, 2 * positions * positions)
    skewed = tiled[:, : positions * (2 * positions - 1)].reshape(
        head_count, positions, 2 * positions - 1
    )
    return (skewed[:, :, :positions], onehot)


def diagonal_sums(d_score, onehot):
    head_count, positions = (d_score.shape[0], d_score.shape[1])
    padded = jnp.pad(d_score, ((0, 0), (0, 0), (0, positions - 1)))
    padded = padded.reshape(head_count, positions * (2 * positions - 1))
    padded = jnp.pad(padded, ((0, 0), (0, positions))).reshape(head_count, positions, 2 * positions)
    column = jnp.sum(padded, axis=1)
    by_dist = jnp.concatenate(
        [jnp.sum(column[:, :positions], axis=1, keepdims=True), column[:, :positions:-1]], axis=1
    )
    return jnp.dot(
        jnp.transpose(onehot, (1, 0)),
        jnp.transpose(by_dist, (1, 0)),
        precision=lax.Precision.HIGHEST,
    )


def scores_of(query, keys, bias, mask):
    rows = query.shape[0]
    q3 = query.reshape(rows, -1, HEAD)
    k3 = keys.reshape(keys.shape[0], -1, HEAD)
    scores = prod("qhd,khd->hqk", q3, k3)
    if bias is not None:
        scores = scores + bias
    if mask is not None:
        scores = jnp.where(mask[None], scores, -1e30)
    return scores


def attend(query, keys, values, bias, mask, shifted):
    rows = query.shape[0]
    scores = scores_of(query, keys, bias, mask)
    if shifted:
        top = jnp.max(scores, axis=-1, keepdims=True)
        lse = top + jnp.log(jnp.sum(jnp.exp(scores - top), axis=-1, keepdims=True))
    else:
        lse = jnp.log(jnp.sum(jnp.exp(scores), axis=-1, keepdims=True))
    prob = jnp.exp(scores - lse).astype(jnp.bfloat16)
    v3 = values.reshape(values.shape[0], -1, HEAD)
    out = prod("hqk,khd->qhd", prob, v3).reshape(rows, -1).astype(jnp.bfloat16)
    return (out, lse)


def attend_back(query, keys, values, out, lse, grad_out, bias, mask):
    rows = query.shape[0]
    scores = scores_of(query, keys, bias, mask)
    prob = jnp.exp(scores - lse)
    prob_b = prob.astype(jnp.bfloat16)
    q3 = query.reshape(rows, -1, HEAD)
    k3 = keys.reshape(keys.shape[0], -1, HEAD)
    v3 = values.reshape(values.shape[0], -1, HEAD)
    grad3 = grad_out.reshape(rows, -1, HEAD)
    grad_b = grad3.astype(jnp.bfloat16)
    out3 = out.reshape(rows, -1, HEAD).astype(jnp.float32)
    d_val = prod("hqk,qhd->khd", prob_b, grad_b)
    d_prob = prod("qhd,khd->hqk", grad_b, v3)
    delta = jnp.transpose(jnp.sum(grad3 * out3, axis=2), (1, 0))
    d_score = prob * (d_prob - delta[:, :, None])
    d_score_b = d_score.astype(jnp.bfloat16)
    d_query = prod("hqk,khd->qhd", d_score_b, k3)
    d_key = prod("hqk,qhd->khd", d_score_b, q3)
    shape_q = (rows, -1)
    shape_k = (keys.shape[0], -1)
    return (
        d_query.reshape(shape_q).astype(jnp.bfloat16),
        d_key.reshape(shape_k).astype(jnp.bfloat16),
        d_val.reshape(shape_k).astype(jnp.bfloat16),
        d_score,
    )


def forward(rows, enc, length, bucket_ids, weights, table):
    qkv_w, out_w, ff_in, ff_out, gains = weights
    positions = rows.shape[0]
    gain_f = gains.astype(jnp.float32)
    start = rows.astype(jnp.float32)
    h1, n1, r1 = rms_fwd(start, gain_f[0])
    qkv = prod("ld,cde->cle", h1, qkv_w[0:3]).astype(jnp.bfloat16)
    row_ids = lax.broadcasted_iota(jnp.int32, (positions, positions), 0)
    col_ids = lax.broadcasted_iota(jnp.int32, (positions, positions), 1)
    mask = (col_ids <= row_ids) & (col_ids < length)
    bias, onehot = toeplitz_bias(bucket_ids, table, positions)
    a1, lse1 = attend(qkv[0], qkv[1], qkv[2], bias, mask, True)
    x1 = start + prod("le,ed->ld", a1, out_w[0])
    h2, n2, r2 = rms_fwd(x1, gain_f[1])
    qc = prod("ld,de->le", h2, qkv_w[3]).astype(jnp.bfloat16)
    kvc = prod("ld,cde->cle", enc, qkv_w[4:6]).astype(jnp.bfloat16)
    ac, lse2 = attend(qc, kvc[0], kvc[1], None, None, False)
    x2 = x1 + prod("le,ed->ld", ac, out_w[1])
    h3, n3, r3 = rms_fwd(x2, gain_f[2])
    gate_up = prod("ld,cdf->clf", h3, ff_in)
    hidden = (gelu_tanh(gate_up[0]) * gate_up[1]).astype(jnp.bfloat16)
    result = x2 + prod("lf,fd->ld", hidden, ff_out)
    saved = (
        h1,
        n1,
        r1,
        qkv,
        bias,
        mask,
        a1,
        lse1,
        h2,
        n2,
        r2,
        qc,
        kvc,
        ac,
        lse2,
        h3,
        n3,
        r3,
        gate_up,
        hidden,
        onehot,
    )
    return (result.astype(jnp.bfloat16), saved)


def ff_back(saved, weights, cot):
    qkv_w, out_w, ff_in, ff_out, gains = weights
    gain_f = gains.astype(jnp.float32)
    h3, n3, r3, gate_up, hidden = (saved[15], saved[16], saved[17], saved[18], saved[19])
    d_ffout = prod("lf,ld->fd", hidden, cot)
    d_hidden = prod("ld,fd->lf", cot, ff_out)
    gelu_val, gelu_pull = jax.vjp(gelu_tanh, gate_up[0])
    d_gate = gelu_pull(d_hidden * gate_up[1])[0]
    d_up = d_hidden * gelu_val
    d_gate_up = jnp.stack([d_gate, d_up]).astype(jnp.bfloat16)
    d_ffin = prod("ld,clf->cdf", h3, d_gate_up)
    d_h3 = prod("clf,cdf->ld", d_gate_up, ff_in)
    back3, gain3 = rms_bwd(d_h3, n3, r3, gain_f[2])
    return (cot.astype(jnp.float32) + back3, d_ffin, d_ffout, gain3)


def cross_back(saved, weights, enc, dx2):
    qkv_w, out_w, ff_in, ff_out, gains = weights
    gain_f = gains.astype(jnp.float32)
    h2, n2, r2, qc, kvc, ac, lse2 = (
        saved[8],
        saved[9],
        saved[10],
        saved[11],
        saved[12],
        saved[13],
        saved[14],
    )
    dx2_b = dx2.astype(jnp.bfloat16)
    d_outc = prod("le,ld->ed", ac, dx2_b)
    d_ac = prod("ld,ed->le", dx2_b, out_w[1])
    d_qc, d_kc, d_vc, unused = attend_back(qc, kvc[0], kvc[1], ac, lse2, d_ac, None, None)
    g_qc = prod("ld,le->de", h2, d_qc)
    d_kvc = jnp.stack([d_kc, d_vc])
    g_kvc = prod("ld,cle->cde", enc, d_kvc)
    enc_grad = prod("cle,cde->ld", d_kvc, qkv_w[4:6]).astype(jnp.bfloat16)
    d_h2 = prod("le,de->ld", d_qc, qkv_w[3])
    back2, gain2 = rms_bwd(d_h2, n2, r2, gain_f[1])
    return (dx2 + back2, g_qc, g_kvc, d_outc, gain2, enc_grad)


def self_back(saved, weights, dx1):
    qkv_w, out_w, ff_in, ff_out, gains = weights
    gain_f = gains.astype(jnp.float32)
    h1, n1, r1, qkv, bias, mask, a1, lse1 = saved[0:8]
    onehot = saved[20]
    dx1_b = dx1.astype(jnp.bfloat16)
    d_outs = prod("le,ld->ed", a1, dx1_b)
    d_a1 = prod("ld,ed->le", dx1_b, out_w[0])
    d_q, d_k, d_v, d_score = attend_back(qkv[0], qkv[1], qkv[2], a1, lse1, d_a1, bias, mask)
    d_qkv = jnp.stack([d_q, d_k, d_v])
    g_qkv = prod("ld,cle->cde", h1, d_qkv)
    d_h1 = prod("cle,cde->ld", d_qkv, qkv_w[0:3])
    back1, gain1 = rms_bwd(d_h1, n1, r1, gain_f[0])
    d_table = diagonal_sums(d_score, onehot)
    return ((dx1 + back1).astype(jnp.bfloat16), g_qkv, d_outs, gain1, d_table)


def to_blocks(array, width):
    blocks = []
    for copy in range(array.shape[0]):
        for start in range(0, array.shape[-1], width):
            block = array[copy, ..., start : start + width]
            short = width - block.shape[-1]
            if short:
                block = jnp.pad(block, ((0, 0),) * (block.ndim - 1) + ((0, short),))
            blocks.append(block)
    return blocks


def from_blocks(blocks, shape, width):
    copies, rows, columns = shape
    each = -(-columns // width)
    planes = []
    for copy in range(copies):
        part = [blocks[copy * each + at] for at in range(each)]
        part[-1] = part[-1][..., : columns - (each - 1) * width]
        planes.append(part[0] if each == 1 else jnp.concatenate(part, axis=-1))
    return planes


def per_device(
    inputs,
    encoded,
    lengths,
    bucket_ids,
    qkv_weights,
    out_weights,
    ff_in,
    ff_out,
    gains,
    bias_table,
    cotangent,
):
    count = lax.axis_size("fsdp")
    shards = (
        jnp.transpose(qkv_weights, (1, 0, 2)),
        jnp.transpose(out_weights, (1, 0, 2)),
        jnp.transpose(ff_in, (1, 0, 2)),
        ff_out[None],
    )
    width = qkv_weights.shape[-1]
    depth = qkv_weights.shape[0]
    tall = ff_out.shape[0]
    blocks = to_blocks(shards[0], width) + to_blocks(shards[1], width) + to_blocks(shards[2], width)
    slots = gains.size
    tail = 8 * -(-slots // (8 * width))
    gain_rows = jnp.pad(gains.reshape(1, slots), ((0, 0), (0, tail * width - slots)))
    packed = jnp.concatenate(blocks + [ff_out, gain_rows.reshape(tail, width)], axis=0)
    whole = lax.all_gather(packed, "fsdp", axis=0, tiled=False)
    cut = len(blocks) * depth
    stacked = whole[:, :cut].reshape(count, len(blocks), depth, width)
    stacked = jnp.transpose(stacked, (1, 0, 2, 3)).reshape(len(blocks), count * depth, width)
    ff_out_all = whole[:, cut : cut + tall].reshape(count * tall, width)
    stacked, ff_out_all = lax.optimization_barrier((stacked, ff_out_all))
    n_qkv, n_out = qkv_weights.shape[1], out_weights.shape[1]
    ff_all = jnp.stack(from_blocks(stacked[n_qkv + n_out :], shards[2].shape, width))
    main = (stacked[:n_qkv], stacked[n_qkv : n_qkv + n_out], ff_all, ff_out_all[None])
    gain_all = whole[:, -tail:].reshape(count, tail * width)[:, :slots]
    gain_all = gain_all.reshape(count, gains.shape[0], gains.shape[1])
    gain_all = jnp.transpose(gain_all, (1, 0, 2)).reshape(gains.shape[0], -1)
    weights = (main[0], main[1], main[2], main[3][0], gain_all)
    result, saved = forward(inputs[0], encoded[0], lengths[0], bucket_ids, weights, bias_table)
    dx2, g_ffin, g_ffout, gain3 = ff_back(saved, weights, cotangent[0])
    dx1, g_qc, g_kvc, g_outc, gain2, enc_grad = cross_back(saved, weights, encoded[0], dx2)
    dx, g_qkvs, g_outs, gain1, g_table = self_back(saved, weights, dx1)
    wide = [g_qkvs[0], g_qkvs[1], g_qkvs[2], g_qc, g_kvc[0], g_kvc[1], g_outs, g_outc]
    wide += to_blocks(g_ffin, width)
    wide.append(g_ffout)
    g_gain = jnp.stack([gain1, gain2, gain3]).reshape(gains.shape[0], count, -1)
    g_gain = jnp.transpose(g_gain, (1, 0, 2)).reshape(count, slots)
    g_gain = jnp.pad(g_gain, ((0, 0), (0, tail * width - slots))).reshape(count, tail, width)
    parts = [grad.astype(jnp.bfloat16).reshape(count, -1, width) for grad in wide]
    send = jnp.concatenate(parts + [g_gain.astype(jnp.bfloat16)], axis=1)
    send, g_table = lax.optimization_barrier((send, g_table))
    own = lax.psum_scatter(send, "fsdp", scatter_dimension=0, tiled=False).astype(jnp.float32)
    mine = own[:cut].reshape(len(blocks), depth, width)
    s_ffin = jnp.stack(from_blocks(mine[n_qkv + n_out :], shards[2].shape, width))
    s_main = (mine[:n_qkv], mine[n_qkv : n_qkv + n_out], s_ffin, own[cut : cut + tall][None])
    s_gain = own[-tail:].reshape(tail * width)[:slots].reshape(gains.shape)
    s_table = lax.psum(g_table, "fsdp")
    return (
        result[None],
        dx[None],
        enc_grad[None],
        jnp.transpose(s_main[0], (1, 0, 2)),
        jnp.transpose(s_main[1], (1, 0, 2)),
        jnp.transpose(s_main[2], (1, 0, 2)),
        s_main[3][0],
        s_gain,
        s_table,
    )


def solution(mesh):
    placed = (
        P("fsdp", None, None),
        P("fsdp", None, None),
        P("fsdp"),
        P(),
        P("fsdp", None, None),
        P("fsdp", None, None),
        P("fsdp", None, None),
        P("fsdp", None),
        P(None, "fsdp"),
        P(),
        P("fsdp", None, None),
    )
    return jax.shard_map(
        per_device,
        mesh=mesh,
        in_specs=placed,
        out_specs=(
            P("fsdp", None, None),
            P("fsdp", None, None),
            P("fsdp", None, None),
            P("fsdp", None, None),
            P("fsdp", None, None),
            P("fsdp", None, None),
            P("fsdp", None),
            P(None, "fsdp"),
            P(),
        ),
        check_vma=False,
    )
```

profile of v0, /device:TPU:0, one launch (start us, length us, event | category | flops | bytes accessed | tf_op | source)
XLA Modules:
  0.0 536.2 jit_solution(1657681668492004055)
XLA Ops:
  19.7 3.4 reshape.321
  25.4 123.4 %all-gather.3.cloned.1.call-done = bf16[13056,768]{1,0:T(8,128)(2,1)} async-done(((bf16[408,768]{1,0:T(8,128)(2,1)}), bf16[13056,768]{1,0:T(8,128)(2,1)}) %all-gather.3.cloned.1.call-update) | async-done | bytes 20054032 | tf_op jit(solution)/shard_map/all_gather | solution.py:282
  148.8 7.9 %slice.390 = bf16[32,336,768]{2,1,0:T(8,128)(2,1)S(1)} slice(bf16[32,408,768]{2,1,0:T(8,128)(2,1)} %bitcast.363), slice={[0:32], [0:336], [0:768]} | slice | bytes 33030144 | tf_op jit(solution)/shard_map/slice | solution.py:284
  156.8 3.9 slice.391
  161.7 6.6 %copy.95 = bf16[14,32,24,768]{3,2,1,0:T(8,128)(2,1)} copy(bf16[14,32,24,768]{3,2,0,1:T(8,128)(2,1)S(1)} %bitcast.362) | data formatting | bytes 33030144 | tf_op jit(solution)/shard_map/transpose | solution.py:285
  168.3 22.3 %copy.96 = bf16[14,768,768]{1,2,0:T(8,128)(2,1)} copy(bf16[14,768,768]{2,1,0:T(8,128)(2,1)} %bitcast.353) | data formatting | bytes 33030144 | tf_op jit(solution)/shard_map/optimization_barrier | solution.py:287
  190.6 3.2 fusion.154
  194.8 3.2 fusion.12
  198.9 1.8 multiply_reduce_fusion.7
  200.7 2.2 fusion.35
  209.2 5.2 slice_bitcast_fusion.5
  216.4 3.0 maximum_bitcast_fusion
  219.4 1.9 fusion.5
  223.0 1.8 multiply_reduce_fusion
  226.7 2.6 multiply_reduce_fusion.1
  231.9 2.1 convolution_convert_fusion.5
  235.3 4.0 fusion.84
  239.3 2.9 convert_bitcast_fusion.1
  246.8 2.1 convert_bitcast_fusion
  249.0 2.2 fusion.155
  254.6 2.3 copy.150
  256.9 2.5 pad.39.clone
  259.3 3.9 reshape.330
  269.1 3.7 fusion.156
  285.5 2.1 pad.38
  287.6 2.4 copy.130
  292.0 2.5 constant_dynamic-update-slice_fusion.30
  308.2 1.9 constant_dynamic-update-slice_fusion.17
  311.9 38.4 %psum.7 = f32[32,12]{0,1:T(8,128)} all-reduce(f32[32,12]{0,1:T(8,128)S(1)} %fusion.123), channel_id=1, replica_groups=mesh['fsdp'=32] {'fsdp'}, use_global_device_ids=true, to_apply=%region_17.18 | all-reduce | flops 384 | bytes 3072 | tf_op jit(solution)/shard_map/psum | solution.py:313
  350.3 3.5 fusion.45
  353.8 1.9 fusion.89
  357.2 166.7 %reduce-scatter.2.cloned.1.call-done = bf16[1,408,768]{2,1,0:T(8,128)(2,1)} async-done(((bf16[32,408,768]{2,1,0:T(8,128)(2,1)}), bf16[1,408,768]{2,1,0:T(8,128)(2,1)}) %reduce-scatter.2.cloned.1.call-update) | async-done | bytes 626704 | tf_op jit(solution)/shard_map/reduce_scatter | solution.py:308
  (279 shorter events, 83.0 us)
Async XLA Ops:
  7.2 193.5 %copy-start = (bf16[1,64,768]{2,1,0:T(8,128)(2,1)S(1)}, bf16[1,64,768]{2,1,0:T(8,128)(2,1)}, u32[]{:S(2)}) copy-start(bf16[1,64,768]{2,1,0:T(8,128)(2,1)} %param.12) | copy-start | bytes 294916
  7.2 141.7 %all-gather.3.cloned.1.call-start = ((), (), s32[]{:S(2)}) async-start(), calls=%async_computation.2 | async-start | bytes 20680704 | tf_op jit(solution)/shard_map/all_gather | solution.py:282
  16.5 507.4 %reduce-scatter.2.cloned.1.call-start = ((), (), s32[]{:S(2)}) async-start(), calls=%async_computation.1 | async-start | bytes 20680704 | tf_op jit(solution)/shard_map/reduce_scatter | solution.py:308
  19.7 5.5 %copy-start.4 = (bf16[1,128,768]{2,1,0:T(8,128)(2,1)S(1)}, bf16[1,128,768]{2,1,0:T(8,128)(2,1)}, u32[]{:S(2)}) copy-start(bf16[1,128,768]{2,1,0:T(8,128)(2,1)} %param.11) | copy-start | bytes 589828
  198.1 4.8 copy-start.34
  198.1 4.8 copy-start.36
  198.1 4.8 copy-start.38
  198.8 6.2 %copy-start.26 = (bf16[12,64,128]{2,1,0:T(8,128)(2,1)}, bf16[12,64,128]{2,1,0:T(8,128)(2,1)S(1)}, u32[]{:S(2)}) copy-start(bf16[12,64,128]{2,1,0:T(8,128)(2,1)S(1)} %convolution_convert_fusion.12) | copy-start | bytes 589828
  203.1 3.7 copy-start.48
  203.3 3.5 copy-start.32
  209.1 15.7 %copy-start.19 = (f32[128,768]{1,0:T(8,128)}, f32[128,768]{1,0:T(8,128)S(1)}, u32[]{:S(2)}) copy-start(f32[128,768]{1,0:T(8,128)S(1)} %get-tuple-element.94) | copy-start | bytes 1179652
  225.6 3.9 copy-start.17
  225.6 3.9 copy-start.27
  226.7 3.7 copy-start.39
  229.4 14.5 %copy-start.2 = (f32[128,768]{1,0:T(8,128)}, f32[128,768]{1,0:T(8,128)S(1)}, u32[]{:S(2)}) copy-start(f32[128,768]{1,0:T(8,128)S(1)} %multiply_add_fusion.3) | copy-start | bytes 1179652
  230.0 4.0 copy-start.31
  230.0 4.0 copy-start.44
  239.3 4.5 copy-start.28
  239.3 6.0 %copy-start.42 = (bf16[12,64,128]{2,1,0:T(8,128)(2,1)S(1)}, bf16[12,64,128]{2,1,0:T(8,128)(2,1)}, u32[]{:S(2)}) copy-start(bf16[12,64,128]{2,1,0:T(8,128)(2,1)} %copy-done.40) | copy-start | bytes 589828
  242.3 4.6 copy-start.20
  242.3 4.6 copy-start.58
  242.3 4.6 copy-start.60
  269.1 4.8 copy-start.64
  292.0 3.6 copy-start.12
  292.0 4.8 copy-start.16
  295.7 3.5 copy-start.11
  311.8 38.5 %copy-start.67 = (f32[128]{0:T(128)S(1)}, f32[128]{0:T(128)}, u32[]{:S(2)}) copy-start(f32[128]{0:T(128)} %get-tuple-element.49) | copy-start | bytes 1540
  311.8 38.5 %copy-start.65 = (bf16[1,64,768]{2,1,0:T(8,128)(2,1)S(1)}, bf16[1,64,768]{2,1,0:T(8,128)(2,1)}, u32[]{:S(2)}) copy-start(bf16[1,64,768]{2,1,0:T(8,128)(2,1)} %copy.124) | copy-start | bytes 294916
  311.8 43.9 %copy-start.63 = (f32[2,128,2048]{1,2,0:T(8,128)S(1)}, f32[2,128,2048]{1,2,0:T(8,128)}, u32[]{:S(2)}) copy-start(f32[2,128,2048]{1,2,0:T(8,128)} %copy-done.61) | copy-start | bytes 6291460
  311.9 41.9 %copy-start.3 = (f32[128,768]{1,0:T(8,128)S(1)}, f32[128,768]{1,0:T(8,128)}, u32[]{:S(2)}) copy-start(f32[128,768]{1,0:T(8,128)} %copy-done.2) | copy-start | bytes 1179652
  311.9 43.8 %copy-start.21 = (f32[128,768]{1,0:T(8,128)S(1)}, f32[128,768]{1,0:T(8,128)}, u32[]{:S(2)}) copy-start(f32[128,768]{1,0:T(8,128)} %copy-done.19) | copy-start | bytes 1179652
  350.3 5.4 %copy-start.23 = (bf16[32,64,768]{2,1,0:T(8,128)(2,1)S(1)}, bf16[32,64,768]{2,1,0:T(8,128)(2,1)}, u32[]{:S(2)}) copy-start(bf16[32,64,768]{2,1,0:T(8,128)(2,1)} %slice.391) | copy-start | bytes 9437188
  (38 other events, 82.6 us)
Sparse Core Ops, SparseCore 0:
  16.6 132.1 all-gather.2
  312.0 211.8 reduce-scatter.1
where the time goes:
time: 538 us; the launch traced here: 536 us
  waiting for transfers between devices  290 us (54%)
  local copies, waits for them, and re-layouts  134 us (25%)
  matrix products  47.5 us (9%)
  blocking collectives  38.4 us (7%)
  between operations  15.8 us (3%)
  other arithmetic  10 us (2%)
    reduce_scatter x1, waiting for transfers between devices, per_device(): lax.psum_scatter(send, 'fsdp', scatter_dimension=0, tiled=False)  167 us
    all_gather x1, waiting for transfers between devices, per_device(): whole = lax.all_gather(packed, 'fsdp', axis=0, tiled=False)  123 us
    dot_general x33, matrix products, prod(): return jnp.einsum(form, left, right, preferred_element_type=jnp.float32)  45.6 us
    psum x1, blocking collectives, per_device(): s_table = lax.psum(g_table, 'fsdp')  38.4 us
    unnamed x174, local copies, waits for them, and re-layouts  36.2 us
    optimization_barrier x1, local copies, waits for them, and re-layouts, per_device(): stacked, ff_out_all = lax.optimization_barrier((stacked, ff_out_all))  22.3 us
  transfers between devices with their start and end apart: 2, of which 2 were waited for; matrix products, arithmetic and copies ran while one was open for 3% of the time, Pallas kernels for 0%

commit v1 on v0

--- a/solution.py
+++ b/solution.py
@@ -1,6 +1,10 @@
+import functools
+
 import jax
 import jax.numpy as jnp
 from jax import lax
+from jax.experimental import pallas as pl
+from jax.experimental.pallas import tpu as pltpu
 from jax.sharding import PartitionSpec as P
 
 HEAD = 64
@@ -251,7 +255,7 @@
     return planes
 
 
-def per_device(
+def plain_device(
     inputs,
     encoded,
     lengths,
@@ -324,34 +328,522 @@
     )
 
 
+def planes_of(array, number):
+    width = array.shape[-1] // number
+    return [array[..., at * width : (at + 1) * width] for at in range(number)]
+
+
+def layer_forward(rows, enc, length, bucket_ids, weights, table):
+    (w_qkv, w_qc, w_kvc), (w_o, w_oc), w_in, w_out, gains = weights
+    positions = rows.shape[0]
+    gain_f = gains.astype(jnp.float32)
+    start = rows.astype(jnp.float32)
+    h1, n1, r1 = rms_fwd(start, gain_f[0])
+    qkv = planes_of(prod("ld,de->le", h1, w_qkv).astype(jnp.bfloat16), 3)
+    row_ids = lax.broadcasted_iota(jnp.int32, (positions, positions), 0)
+    col_ids = lax.broadcasted_iota(jnp.int32, (positions, positions), 1)
+    mask = (col_ids <= row_ids) & (col_ids < length)
+    bias, onehot = toeplitz_bias(bucket_ids, table, positions)
+    a1, lse1 = attend(qkv[0], qkv[1], qkv[2], bias, mask, True)
+    x1 = start + prod("le,ed->ld", a1, w_o)
+    h2, n2, r2 = rms_fwd(x1, gain_f[1])
+    qc = prod("ld,de->le", h2, w_qc).astype(jnp.bfloat16)
+    kvc = planes_of(prod("ld,de->le", enc, w_kvc).astype(jnp.bfloat16), 2)
+    ac, lse2 = attend(qc, kvc[0], kvc[1], None, None, False)
+    x2 = x1 + prod("le,ed->ld", ac, w_oc)
+    h3, n3, r3 = rms_fwd(x2, gain_f[2])
+    gate_up = planes_of(prod("ld,df->lf", h3, w_in), 2)
+    hidden = (gelu_tanh(gate_up[0]) * gate_up[1]).astype(jnp.bfloat16)
+    result = x2 + prod("lf,fd->ld", hidden, w_out)
+    saved = (h1, n1, r1, qkv, bias, mask, a1, lse1, h2, n2, r2, qc, kvc, ac, lse2, h3, n3, r3)
+    return (result.astype(jnp.bfloat16), saved + (gate_up, hidden, onehot))
+
+
+def layer_back(saved, weights, enc, cot):
+    (w_qkv, w_qc, w_kvc), (w_o, w_oc), w_in, w_out, gains = weights
+    gain_f = gains.astype(jnp.float32)
+    (h1, n1, r1, qkv, bias, mask, a1, lse1, h2, n2, r2, qc, kvc, ac, lse2, h3, n3, r3) = saved[:18]
+    gate_up, hidden, onehot = saved[18:]
+    g_out = prod("lf,ld->fd", hidden, cot)
+    d_hidden = prod("ld,fd->lf", cot, w_out)
+    gelu_val, gelu_pull = jax.vjp(gelu_tanh, gate_up[0])
+    d_gate = gelu_pull(d_hidden * gate_up[1])[0]
+    d_gate_up = jnp.concatenate([d_gate, d_hidden * gelu_val], axis=1).astype(jnp.bfloat16)
+    g_in = prod("ld,lf->df", h3, d_gate_up)
+    back3, gain3 = rms_bwd(prod("lf,df->ld", d_gate_up, w_in), n3, r3, gain_f[2])
+    dx2 = cot.astype(jnp.float32) + back3
+    dx2_b = dx2.astype(jnp.bfloat16)
+    g_oc = prod("le,ld->ed", ac, dx2_b)
+    d_ac = prod("ld,ed->le", dx2_b, w_oc)
+    d_qc, d_kc, d_vc, unused = attend_back(qc, kvc[0], kvc[1], ac, lse2, d_ac, None, None)
+    g_qc = prod("ld,le->de", h2, d_qc)
+    d_kvc = jnp.concatenate([d_kc, d_vc], axis=1)
+    g_kvc = prod("ld,le->de", enc, d_kvc)
+    enc_grad = prod("le,de->ld", d_kvc, w_kvc).astype(jnp.bfloat16)
+    back2, gain2 = rms_bwd(prod("le,de->ld", d_qc, w_qc), n2, r2, gain_f[1])
+    dx1 = dx2 + back2
+    dx1_b = dx1.astype(jnp.bfloat16)
+    g_o = prod("le,ld->ed", a1, dx1_b)
+    d_a1 = prod("ld,ed->le", dx1_b, w_o)
+    d_q, d_k, d_v, d_score = attend_back(qkv[0], qkv[1], qkv[2], a1, lse1, d_a1, bias, mask)
+    d_qkv = jnp.concatenate([d_q, d_k, d_v], axis=1)
+    g_qkv = prod("ld,le->de", h1, d_qkv)
+    back1, gain1 = rms_bwd(prod("le,de->ld", d_qkv, w_qkv), n1, r1, gain_f[0])
+    d_table = diagonal_sums(d_score, onehot)
+    grads = [g_qkv, g_o, g_qc, g_kvc, g_oc, g_in, g_out]
+    return ((dx1 + back1).astype(jnp.bfloat16), enc_grad, grads, (gain1, gain2, gain3), d_table)
+
+
+MESH = pl.DeviceIdType.MESH
+SUB = 8
+
+
+def place(count):
+    me = lax.axis_index("fsdp")
+    core = lax.rem(me, 2)
+    x = lax.rem(me // 2, 2)
+    y = lax.rem(me // 4, 2)
+    z = me // 8
+    return me, core, x, y, z
+
+
+def device(z, y, x, core):
+    return ((z * 2 + y) * 2 + x) * 2 + core
+
+
+def greet(peers):
+    barrier = pltpu.get_barrier_semaphore()
+    total = 0
+    for cond, peer in peers:
+
+        def signal(peer=peer):
+            pl.semaphore_signal(barrier, inc=1, device_id=(peer,), device_id_type=MESH)
+
+        if cond is None:
+            signal()
+            total = total + 1
+        else:
+            pl.when(cond)(signal)
+            total = total + cond.astype(jnp.int32)
+    pl.semaphore_wait(barrier, total)
+
+
+def both(first, second):
+    if first is None:
+        return second
+    if second is None:
+        return first
+    return jnp.logical_and(first, second)
+
+
+class Sender:
+    def __init__(self, sems):
+        self.sems = sems
+        self.used = 0
+        self.open = []
+
+    def start(self, src, dst, recv, target, cond=None):
+        copy = pltpu.make_async_remote_copy(
+            src_ref=src,
+            dst_ref=dst,
+            send_sem=self.sems.at[self.used],
+            recv_sem=recv,
+            device_id=(target,),
+            device_id_type=MESH,
+        )
+        self.used += 1
+        self.open.append((cond, copy))
+        if cond is None:
+            copy.start()
+        else:
+            pl.when(cond)(copy.start)
+
+    def finish(self):
+        for cond, copy in self.open:
+            if cond is None:
+                copy.wait_send()
+            else:
+                pl.when(cond)(copy.wait_send)
+
+
+def gather_kernel(planes, groups, *refs):
+    ins, outs = refs[:groups], refs[groups : 2 * groups]
+    local_sem, send_sem, recv_sem = refs[2 * groups :]
+    me, core, x, y, z = place(planes)
+    partner, across, along = device(z, y, x, 1 - core), device(z, y, 1 - x, core), device(z, 1 - y, x, core)
+    up, down = device(z + 1, y, x, core), device(z - 1, y, x, core)
+    can_up, can_down = z < planes - 1, z > 0
+    half = planes // 2
+    greet([(None, partner), (None, across), (None, along), (can_up, up), (can_down, down)])
+    sender = Sender(send_sem)
+
+    def arrive(g, src, cond):
+        copy = pltpu.make_async_remote_copy(
+            src_ref=outs[g].at[src],
+            dst_ref=outs[g].at[src],
+            send_sem=send_sem.at[0],
+            recv_sem=recv_sem.at[g, src],
+            device_id=(partner,),
+            device_id_type=MESH,
+        )
+        if cond is None:
+            copy.wait_recv()
+        else:
+            pl.when(cond)(copy.wait_recv)
+
+    def send(g, src, target, cond, own=False):
+        sender.start(
+            ins[g] if own else outs[g].at[src], outs[g].at[src], recv_sem.at[g, src], target, cond
+        )
+
+    def steps(k):
+        if k == 0:
+            return [(None, z)]
+        return [(z - k >= 0, z - k), (z + k < planes, z + k)]
+
+    def line(k):
+        for g in range(groups):
+            for side, (cond, zs) in enumerate(steps(k)):
+                src = device(zs, y, x, core)
+                if k:
+                    arrive(g, src, cond)
+                if k == 0 or side == 0:
+                    send(g, src, up, both(cond, can_up), k == 0)
+                if k == 0 or side == 1:
+                    send(g, src, down, both(cond, can_down), k == 0)
+                send(g, src, across, cond, k == 0)
+                send(g, src, along, cond, k == 0)
+                send(g, src, partner, cond, k == 0)
+
+    def plane(k):
+        for g in range(groups):
+            for cond, zs in steps(k):
+                src = device(zs, y, 1 - x, core)
+                arrive(g, src, cond)
+                send(g, src, along, both(cond, zs >= half))
+                send(g, src, partner, cond)
+                src = device(zs, 1 - y, x, core)
+                arrive(g, src, cond)
+                send(g, src, across, both(cond, zs < half))
+                send(g, src, partner, cond)
+
+    def corner(k):
+        for g in range(groups):
+            for cond, zs in steps(k):
+                src = device(zs, 1 - y, 1 - x, core)
+                arrive(g, src, cond)
+                send(g, src, partner, cond)
+
+    line(0)
+    for g in range(groups):
+        pltpu.make_async_copy(ins[g], outs[g].at[me], local_sem.at[g]).start()
+    for k in range(planes):
+        if k + 1 < planes:
+            line(k + 1)
+        plane(k)
+        if k:
+            corner(k - 1)
+    corner(planes - 1)
+    for g in range(groups):
+        for zs in range(planes):
+            for ys in range(2):
+                for xs in range(2):
+                    arrive(g, device(zs, ys, xs, 1 - core), None)
+    sender.finish()
+    for g in range(groups):
+        pltpu.make_async_copy(ins[g], outs[g].at[me], local_sem.at[g]).wait()
+
+
+def gather(shards, count):
+    planes, groups = count // 8, len(shards)
+    sites = groups * (5 + (planes - 1) * 8 + (2 * planes - 1) * 5)
+    spec = pl.BlockSpec(memory_space=pl.ANY)
+    return pl.pallas_call(
+        functools.partial(gather_kernel, planes, groups),
+        out_shape=tuple(jax.ShapeDtypeStruct((count,) + s.shape, s.dtype) for s in shards),
+        in_specs=[spec] * groups,
+        out_specs=tuple([spec] * groups),
+        scratch_shapes=[
+            pltpu.SemaphoreType.DMA((groups,)),
+            pltpu.SemaphoreType.DMA((sites,)),
+            pltpu.SemaphoreType.DMA((groups, count)),
+        ],
+        compiler_params=pltpu.CompilerParams(collective_id=0, has_side_effects=True),
+        name="gather",
+    )(*shards)
+
+
+def scatter_kernel(planes, groups, *refs):
+    grads, small = refs[:groups], refs[groups]
+    outs, small_out = refs[groups + 1 : 2 * groups + 1], refs[2 * groups + 1]
+    rest = refs[2 * groups + 2 :]
+    mine, theirs, from_x, from_y, line_x, line_y, line_u, line_d = (
+        rest[i * groups : (i + 1) * groups] for i in range(8)
+    )
+    held, got, local_sem, send_sem, pair_sem, half_sem, line_sem, chain_sem, small_sem = rest[8 * groups :]
+    me, core, x, y, z = place(planes)
+    partner, across, along = device(z, y, x, 1 - core), device(z, y, 1 - x, core), device(z, 1 - y, x, core)
+    up, down = device(z + 1, y, x, core), device(z - 1, y, x, core)
+    can_up, can_down = z < planes - 1, z > 0
+    half = planes // 2
+    others = [device(lax.rem(z + k, planes), y, x, core) for k in range(1, planes)]
+    greet([(None, p) for p in (partner, across, along, *others)])
+    sender = Sender(send_sem)
+
+    def wait(dst, sem, cond=None):
+        copy = pltpu.make_async_remote_copy(
+            src_ref=dst,
+            dst_ref=dst,
+            send_sem=send_sem.at[0],
+            recv_sem=sem,
+            device_id=(partner,),
+            device_id_type=MESH,
+        )
+        if cond is None:
+            copy.wait_recv()
+        else:
+            pl.when(cond)(copy.wait_recv)
+
+    lines = [(1 - y, 1 - x), (y, 1 - x), (1 - y, x), (y, x)]
+
+    def local(g):
+        return pltpu.make_async_copy(grads[g].at[:, :, :, core], mine[g], local_sem.at[g])
+
+    for g in range(groups):
+        local(g).start()
+    for at, (ys, xs) in enumerate(lines):
+        for g in range(groups):
+            sender.start(
+                grads[g].at[:, ys, xs, 1 - core], theirs[g].at[:, ys, xs], pair_sem.at[g, at], partner
+            )
+
+    def add(g, ys, xs, low, high, terms):
+        depth = mine[g].shape[3]
+
+        def body(i, carry):
+            zs, r = low + i // depth, lax.rem(i, depth)
+            total = mine[g][zs, ys, xs, r].astype(jnp.float32)
+            for term in terms:
+                total = total + term(zs, r).astype(jnp.float32)
+            mine[g][zs, ys, xs, r] = total.astype(jnp.bfloat16)
+            return carry
+
+        lax.fori_loop(0, (high - low) * depth, body, 0)
+
+    def pair(g, ys, xs):
+        return lambda zs, r: theirs[g][zs, ys, xs, r]
+
+    held[0] = small[...]
+    for r, peer in enumerate((partner, across, along)):
+        sender.start(held.at[r], got.at[r], small_sem.at[r], peer)
+
+        wait(got.at[r], small_sem.at[r])
+        held[r + 1] = held[r] + got[r]
+    for peer in others:
+        sender.start(held.at[3], got.at[3 + z], small_sem.at[3 + z], peer)
+
+    ys, xs = lines[0]
+    for g in range(groups):
+        local(g).wait()
+        wait(theirs[g].at[:, ys, xs], pair_sem.at[g, 0])
+        add(g, ys, xs, 0, half, [pair(g, ys, xs)])
+        sender.start(mine[g].at[pl.ds(0, half), ys, xs], from_x[g], half_sem.at[g, 0], across)
+        add(g, ys, xs, half, planes, [pair(g, ys, xs)])
+        sender.start(
+            mine[g].at[pl.ds(half, planes - half), ys, xs], from_y[g], half_sem.at[g, 1], along
+        )
+    low, high = pl.ds(0, half), pl.ds(half, planes - half)
+    for g in range(groups):
+        ys, xs = lines[1]
+        wait(theirs[g].at[:, ys, xs], pair_sem.at[g, 1])
+        add(g, ys, xs, 0, half, [pair(g, ys, xs)])
+        sender.start(mine[g].at[low, ys, xs], line_x[g].at[low], line_sem.at[g, 0], across)
+        ys, xs = lines[2]
+        wait(theirs[g].at[:, ys, xs], pair_sem.at[g, 2])
+        add(g, ys, xs, half, planes, [pair(g, ys, xs)])
+        sender.start(mine[g].at[high, ys, xs], line_y[g].at[high], line_sem.at[g, 3], along)
+    for g in range(groups):
+        ys, xs = lines[1]
+        wait(from_y[g], half_sem.at[g, 1])
+        add(g, ys, xs, half, planes, [pair(g, ys, xs), lambda zs, r, g=g: from_y[g][zs - half, r]])
+        sender.start(mine[g].at[high, ys, xs], line_x[g].at[high], line_sem.at[g, 1], across)
+        ys, xs = lines[2]
+        wait(from_x[g], half_sem.at[g, 0])
+        add(g, ys, xs, 0, half, [pair(g, ys, xs), lambda zs, r, g=g: from_x[g][zs, r]])
+        sender.start(mine[g].at[low, ys, xs], line_y[g].at[low], line_sem.at[g, 2], along)
+    for g in range(groups):
+        wait(theirs[g].at[:, y, x], pair_sem.at[g, 3])
+        wait(line_x[g].at[low], line_sem.at[g, 0])
+        wait(line_x[g].at[high], line_sem.at[g, 1])
+        wait(line_y[g].at[low], line_sem.at[g, 2])
+        wait(line_y[g].at[high], line_sem.at[g, 3])
+        add(
+            g, y, x, 0, planes,
+            [pair(g, y, x), lambda zs, r, g=g: line_x[g][zs, r], lambda zs, r, g=g: line_y[g][zs, r]],
+        )
+        for k in range(planes - 1, 0, -1):
+            chain(g, k, wait, sender, mine, (line_u, line_d), chain_sem, (y, x, z, planes), (up, down))
+    for g in range(groups):
+        wait(line_u[g].at[z], chain_sem.at[g, 0, z], can_down)
+        wait(line_d[g].at[z], chain_sem.at[g, 1, z], can_up)
+        depth = mine[g].shape[3]
+        zero = jnp.zeros(mine[g].shape[4:], jnp.float32)
+
+        def body(r, carry, g=g):
+            total = mine[g][z, y, x, r].astype(jnp.float32)
+            total = total + jnp.where(can_down, line_u[g][z, r].astype(jnp.float32), zero)
+            total = total + jnp.where(can_up, line_d[g][z, r].astype(jnp.float32), zero)
+            outs[g][r] = total
+            return carry
+
+        lax.fori_loop(0, depth, body, 0)
+    for k in range(1, planes):
+        at = lax.rem(z + k, planes)
+        wait(got.at[3 + at], small_sem.at[3 + at])
+    got[3 + z] = held[3]
+    total = got[3]
+    for zs in range(1, planes):
+        total = total + got[3 + zs]
+    small_out[...] = total
+    sender.finish()
+
+
+def chain(g, k, wait, sender, mine, lines, sems, where, targets):
+    y, x, z, planes = where
+    for way, (at, inside, fed) in enumerate(
+        ((z + k, z + k < planes, z > 0), (z - k, z - k >= 0, z < planes - 1))
+    ):
+        spot = jnp.clip(at, 0, planes - 1)
+        join = both(inside, fed)
+
+        @pl.when(join)
+        def _(way=way, spot=spot):
+            wait(lines[way][g].at[spot], sems.at[g, way, spot])
+            depth = mine[g].shape[3]
+
+            def body(r, carry):
+                total = mine[g][spot, y, x, r].astype(jnp.float32) + lines[way][g][spot, r].astype(jnp.float32)
+                mine[g][spot, y, x, r] = total.astype(jnp.bfloat16)
+                return carry
+
+            lax.fori_loop(0, depth, body, 0)
+
+        sender.start(mine[g].at[spot, y, x], lines[way][g].at[spot], sems.at[g, way, spot], targets[way], inside)
+
+
+def scatter(grads, small, count):
+    planes, groups = count // 8, len(grads)
+    half = planes // 2
+    blocks = [g.shape[4:] for g in grads]
+    any_spec, vmem = pl.BlockSpec(memory_space=pl.ANY), pl.BlockSpec(memory_space=pltpu.VMEM)
+    sites = groups * (4 + 2 + 4 + 2 * (planes - 1)) + 3 + planes
+
+    def room(*lead):
+        return [pltpu.VMEM(lead + b, jnp.bfloat16) for b in blocks]
+
+    return pl.pallas_call(
+        functools.partial(scatter_kernel, planes, groups),
+        out_shape=tuple(jax.ShapeDtypeStruct(b, jnp.float32) for b in blocks)
+        + (jax.ShapeDtypeStruct(small.shape, jnp.float32),),
+        in_specs=[any_spec] * groups + [vmem],
+        out_specs=tuple([vmem] * (groups + 1)),
+        scratch_shapes=room(planes, 2, 2)
+        + room(planes, 2, 2)
+        + room(half)
+        + room(planes - half)
+        + room(planes) * 1
+        + room(planes)
+        + room(planes)
+        + room(planes)
+        + [
+            pltpu.VMEM((4,) + small.shape, jnp.float32),
+            pltpu.VMEM((3 + planes,) + small.shape, jnp.float32),
+            pltpu.SemaphoreType.DMA((groups,)),
+            pltpu.SemaphoreType.DMA((sites,)),
+            pltpu.SemaphoreType.DMA((groups, 4)),
+            pltpu.SemaphoreType.DMA((groups, 2)),
+            pltpu.SemaphoreType.DMA((groups, 4)),
+            pltpu.SemaphoreType.DMA((groups, 2, planes)),
+            pltpu.SemaphoreType.DMA((3 + planes,)),
+        ],
+        compiler_params=pltpu.CompilerParams(
+            collective_id=1, has_side_effects=True, vmem_limit_bytes=60 * 1024 * 1024
+        ),
+        name="scatter",
+    )(*grads, small)
+
+
+def per_device(
+    inputs, encoded, lengths, bucket_ids, qkv_weights, out_weights, ff_in, ff_out, gains, bias_table, cotangent
+):
+    count = lax.axis_size("fsdp")
+    me = lax.axis_index("fsdp")
+    depth, width, hidden = qkv_weights.shape[0], qkv_weights.shape[-1], ff_in.shape[-1]
+    tall = ff_out.shape[0]
+    pairs = [
+        qkv_weights[:, 0:3].reshape(depth, 3 * width),
+        out_weights[:, 0],
+        qkv_weights[:, 3],
+        qkv_weights[:, 4:6].reshape(depth, 2 * width),
+        out_weights[:, 1],
+        ff_in.reshape(depth, 2 * hidden),
+        ff_out,
+    ]
+    gain_row = lax.dynamic_update_slice(
+        jnp.zeros((SUB, width), jnp.bfloat16), gains, (jnp.int32(0), me * gains.shape[1])
+    )
+    shards = [gain_row] + pairs
+    shards = [s.reshape(-1, SUB, s.shape[-1]) for s in shards]
+    got = gather(shards, count)
+    gain_all = jnp.sum(got[0].astype(jnp.float32), axis=(0, 1))[: gains.shape[0]].astype(jnp.bfloat16)
+    w_qkv, w_o, w_qc, w_kvc, w_oc, w_in, w_out = (w.reshape(-1, w.shape[-1]) for w in got[1:])
+
+    qkv_w = [w_qkv, w_qc, w_kvc]
+    weights = (qkv_w, (w_o, w_oc), w_in, w_out, gain_all)
+    result, saved = layer_forward(inputs[0], encoded[0], lengths[0], bucket_ids, weights, bias_table)
+    dx, enc_grad, grads, (gain1, gain2, gain3), g_table = layer_back(
+        saved, weights, encoded[0], cotangent[0]
+    )
+    planes = count // 8
+    parts = [
+        g.astype(jnp.bfloat16).reshape(planes, 2, 2, 2, -1, SUB, g.shape[-1]) for g in grads
+    ]
+    lanes = 128
+    flat = jnp.concatenate([jnp.stack([gain1, gain2, gain3]).reshape(-1), g_table.reshape(-1)])
+    rows = SUB * -(-flat.size // (SUB * lanes))
+    small = jnp.pad(flat, (0, rows * lanes - flat.size)).reshape(rows, lanes)
+    own = scatter(parts, small, count)
+    total = own[-1].reshape(-1)
+    o_qkv, o_o, o_qc, o_kvc, o_oc, o_in, o_out = (o.reshape(-1, o.shape[-1]) for o in own[:-1])
+    s_gain = total[: gains.shape[0] * width].reshape(gains.shape[0], width)
+    s_gain = lax.dynamic_slice(s_gain, (jnp.int32(0), me * gains.shape[1]), gains.shape)
+    s_table = total[gains.shape[0] * width : flat.size].reshape(bias_table.shape)
+    return (
+        result[None],
+        dx[None],
+        enc_grad[None],
+        jnp.concatenate([o_qkv, o_qc, o_kvc], axis=1).reshape(qkv_weights.shape),
+        jnp.concatenate([o_o, o_oc], axis=1).reshape(out_weights.shape),
+        o_in.reshape(ff_in.shape),
+        o_out,
+        s_gain,
+        s_table,
+    )
+
+
 def solution(mesh):
-    placed = (
-        P("fsdp", None, None),
-        P("fsdp", None, None),
-        P("fsdp"),
-        P(),
-        P("fsdp", None, None),
-        P("fsdp", None, None),
-        P("fsdp", None, None),
-        P("fsdp", None),
-        P(None, "fsdp"),
-        P(),
-        P("fsdp", None, None),
-    )
+    count = mesh.shape["fsdp"]
+
+    def layer(*args):
+        depth, tall = args[4].shape[0], args[7].shape[0]
+        tiled = depth % SUB == 0 and tall % SUB == 0 and count % 8 == 0 and count > 8
+        return (per_device if tiled else plain_device)(*args)
+
+    rows, split = P("fsdp", None, None), P("fsdp", None)
     return jax.shard_map(
-        per_device,
+        layer,
         mesh=mesh,
-        in_specs=placed,
-        out_specs=(
-            P("fsdp", None, None),
-            P("fsdp", None, None),
-            P("fsdp", None, None),
-            P("fsdp", None, None),
-            P("fsdp", None, None),
-            P("fsdp", None, None),
-            P("fsdp", None),
-            P(None, "fsdp"),
-            P(),
-        ),
+        in_specs=(rows, rows, P("fsdp"), P(), rows, rows, rows, split, P(None, "fsdp"), P(), rows),
+        out_specs=(rows, rows, rows, rows, rows, rows, split, P(None, "fsdp"), P()),
         check_vma=False,
     )

time: 538 us -> 313 us (0.58)
  waiting for transfers between devices: 290 us -> 0 us
  Pallas kernels: 0 us -> 225 us
  local copies, waits for them, and re-layouts: 134 us -> 33.6 us
  blocking collectives: 38.4 us -> 0 us
  between operations: 15.8 us -> 2.36 us
    pallas_call x0 -> x2, Pallas kernels: none -> 225 us  [the longest x1 129 us: scatter(): pl.pallas_call(functools.partial(scatter_kernel, planes, groups), out_sha...]
    reduce_scatter x1 -> x0, waiting for transfers between devices: 167 us -> none  [per_device(): lax.psum_scatter(send, 'fsdp', scatter_dimension=0, tiled=False)]
    all_gather x1 -> x0, waiting for transfers between devices: 123 us -> none  [per_device(): whole = lax.all_gather(packed, 'fsdp', axis=0, tiled=False)]
    psum x1 -> x0, blocking collectives: 38.4 us -> none  [per_device(): s_table = lax.psum(g_table, 'fsdp')]
    unnamed x174 -> x115, local copies, waits for them, and re-layouts: 36.2 us -> 7.95 us
    slice x25 -> x12, local copies, waits for them, and re-layouts: 28.6 us -> 3.57 us  [the longest x1 1.09 us: per_device(): out_weights[:, 1]]
    optimization_barrier x1 -> x0, local copies, waits for them, and re-layouts: 22.3 us -> none  [per_device(): stacked, ff_out_all = lax.optimization_barrier((stacked, ff_out_all))]
    transpose x2 -> x0, local copies, waits for them, and re-layouts: 8 us -> none  [the longest x1 6.58 us: per_device(): jnp.transpose(stacked, (1, 0, 2, 3))]
  transfers between devices with their start and end apart: 2 -> 0, of which waited for: 2 -> 0; matrix products, arithmetic and copies ran while one was open for 3% -> 0% of each run, Pallas kernels for 0% -> 0%
where the time goes in v1:
time: 313 us
  Pallas kernels  225 us (72%)
  matrix products  45 us (14%)
  local copies, waits for them, and re-layouts  33.6 us (11%)
  other arithmetic  6.1 us (2%)
    pallas_call x1, Pallas kernels, scatter(): pl.pallas_call(functools.partial(scatter_kernel, planes, groups), out_sha...  129 us
    pallas_call x1, Pallas kernels, gather(): pl.pallas_call(functools.partial(gather_kernel, planes, groups), out_shap...  97 us
    dot_general x33, matrix products, prod(): return jnp.einsum(form, left, right, preferred_element_type=jnp.float32)  44.6 us
    unnamed x115, local copies, waits for them, and re-layouts  7.95 us

profile of v1, /device:TPU:0, one launch (start us, length us, event | category | flops | bytes accessed | tf_op | source)
XLA Modules:
  0.0 312.6 jit_solution(6165710754735689260)
XLA Ops:
  0.7 1.6 dynamic_update_slice.4.refs_0_
  4.0 1.1 fusion.100
  5.8 1.4 slice_bitcast_fusion.refs_3_
  8.8 1.7 reshape_reshape.14.refs_6_
  10.5 97.0 %gather.1 = (bf16[32,1,8,768]{3,2,1,0:T(8,128)(2,1)}, bf16[32,3,8,2304]{3,2,1,0:T(8,128)(2,1)}, bf16[32,3,8,768]{3,2,1,0:T(8,128)(2,1)}, bf16[32,3,8,768]{3,2,1,...) custom-call(bf16[1,8,768]{2,1,0:T(8,128)(2,1)} %copy-done.48, ...), custom_call_target="tpu_custom_call" | custom-call | tf_op jit(solution)/shard_map/gather/pallas_call | solution.py:561
  107.5 1.1 reduce
  108.8 2.7 convolution_convert_fusion.2
  112.8 1.2 copy.109
  114.1 3.4 %reshape.277 = f32[12,128,255]{2,1,0:T(8,128)} reshape(f32[12,32640]{1,0:T(8,128)S(1)} %slice.109) | data formatting | bytes 3133440 | tf_op jit(solution)/shard_map/reshape | solution.py:53
  117.5 1.1 slice-done.2
  124.4 1.0 fusion.102
  125.4 1.5 convolution_convert_fusion.15
  127.4 4.2 %fusion.97 = f32[128,4096]{1,0:T(8,128)S(1)} fusion(bf16[768,4096]{1,0:T(8,128)(2,1)} %bitcast.196, f32[128,768]{1,0:T(8,128)S(1)} %get-tuple-element.92, f32[768]{0:T(1024)S(1)} %get-tuple-element.74, f32[128]{0:T(128)S(1)} %add_rsqrt_fusion), kind=kOutput, calls=%fused_computation.166 | convolution fusion | flops 805601280 | bytes 8785408 | tf_op jit(solution)/shard_map/ld,df->lf/dot_general | solution.py:17
  131.6 1.8 fusion.15
  133.4 1.3 fusion.10
  134.8 2.3 multiply_reduce_fusion
  143.1 1.2 copy-done.9
  144.3 1.4 fusion.32
  146.7 2.2 convolution_convert_fusion.9
  149.1 3.3 %fusion.11 = bf16[1,64,768]{2,1,0:T(8,128)(2,1)} fusion(bf16[768,1536]{1,0:T(8,128)(2,1)} %bitcast.202, bf16[64,768]{0,1:T(8,128)(2,1)} %bitcast.246, bf16[64,768]{0,1:T(8,128)(2,1)S(1)} %bitcast.224), kind=kOutput, calls=%fused_computation.42 | convolution fusion | flops 151437312 | bytes 2654208 | tf_op jit(solution)/shard_map/le,de->ld/dot_general | solution.py:17
  152.4 3.0 convolution_convert_fusion.1
  155.5 1.5 convolution_convert_fusion.8
  156.9 1.6 convolution_convert_fusion.7
  158.5 2.2 convolution_convert_fusion.3
  160.7 1.5 convolution_convert_fusion.6
  162.3 4.5 %convolution_convert_fusion = bf16[768,4096]{1,0:T(8,128)(2,1)} fusion(bf16[128,2048]{1,0:T(8,128)(2,1)S(1)} %copy-done.45, bf16[128,2048]{1,0:T(8,128)(2,1)S(1)} %copy-done.43, f32[128,768]{1,0:T(8,128)S(1)} %get-tuple-element.92, f32[768]{0:T(1024)S(1)} %get-tuple-element.74, f32[128]{0:T(128)S(1)} %add_rsqrt_fusion), kind=kOutput, calls=%fused_computation.1 | convolution fusion | flops 810844160 | bytes 7736832 | tf_op jit(solution)/shard_map/ld,lf->df/dot_general | solution.py:17
  166.8 2.7 convolution_convert_fusion.4
  169.8 1.3 pad.12.clone
  171.1 2.5 reshape.295
  176.2 128.5 %scatter.1 = (f32[3,8,2304]{2,1,0:T(8,128)}, f32[3,8,768]{2,1,0:T(8,128)}, f32[3,8,768]{2,1,0:T(8,128)}, f32[3,8,1536]{2,1,0:T(8,128)}, f32[3,8,768]{2,1,0:T(8,1...) custom-call(bf16[4,2,2,2,3,8,2304]{6,5,4,3,2,1,0:T(8,128)(2,1)} %bitcast.195, ...), custom_call_target="tpu_custom_call" | custom-call | tf_op jit(solution)/shard_map/scatter/pallas_call | solution.py:744
  304.7 1.1 pad_maximum_fusion.4
  309.4 1.1 reshape_reshape.15
  (195 shorter events, 26.1 us)
Async XLA Ops:
  0.6 120.9 %copy-start = (bf16[1,64,768]{2,1,0:T(8,128)(2,1)S(1)}, bf16[1,64,768]{2,1,0:T(8,128)(2,1)}, u32[]{:S(2)}) copy-start(bf16[1,64,768]{2,1,0:T(8,128)(2,1)} %param.12) | copy-start | bytes 294916
  0.7 108.0 %copy-start.2 = (bf16[1,128,768]{2,1,0:T(8,128)(2,1)S(1)}, bf16[1,128,768]{2,1,0:T(8,128)(2,1)}, u32[]{:S(2)}) copy-start(bf16[1,128,768]{2,1,0:T(8,128)(2,1)} %param.11) | copy-start | bytes 589828
  2.3 8.2 %copy-start.48 = (bf16[1,8,768]{2,1,0:T(8,128)(2,1)}, bf16[1,8,768]{2,1,0:T(8,128)(2,1)S(1)}, u32[]{:S(2)}) copy-start(bf16[1,8,768]{2,1,0:T(8,128)(2,1)S(1)} %dynamic_update_slice.4.refs_0_) | copy-start | bytes 36868
  108.8 2.9 copy-start.50
  108.8 2.9 copy-start.51
  111.7 8.9 %copy-start.22 = (bf16[128,768]{0,1:T(8,128)(2,1)}, bf16[128,768]{0,1:T(8,128)(2,1)S(1)}, u32[]{:S(2)}) copy-start(bf16[128,768]{0,1:T(8,128)(2,1)S(1)} %copy.74) | copy-start | bytes 589828
  124.2 2.7 copy-start.7
  126.9 11.0 %copy-start.18 = (bf16[12,64,128]{2,1,0:T(8,128)(2,1)}, bf16[12,64,128]{2,1,0:T(8,128)(2,1)S(1)}, u32[]{:S(2)}) copy-start(bf16[12,64,128]{2,1,0:T(8,128)(2,1)S(1)} %convolution_convert_fusion.15) | copy-start | bytes 589828
  127.3 4.2 %copy-start.10 = (bf16[32,8,8,768]{3,2,1,0:T(8,128)(2,1)S(1)}, bf16[32,8,8,768]{3,2,1,0:T(8,128)(2,1)}, u32[]{:S(2)}) copy-start(bf16[32,8,8,768]{3,2,1,0:T(8,128)(2,1)} %get-tuple-element.32) | copy-start | bytes 9437188
  127.4 4.2 %copy-start.39 = (bf16[1,128,768]{2,1,0:T(8,128)(2,1)S(1)}, bf16[1,128,768]{2,1,0:T(8,128)(2,1)}, u32[]{:S(2)}) copy-start(bf16[1,128,768]{2,1,0:T(8,128)(2,1)} %param.21) | copy-start | bytes 589828
  127.4 7.4 %slice-start = ((s8[6291456]{0:T(1024)(128)(4,1)}), s8[4194304]{0:T(1024)(128)(4,1)S(1)}, s32[]{:S(2)}) async-start(s8[6291456]{0:T(1024)(128)(4,1)} %bitcast.197), calls=%async_computation | async-start | bytes 8388608
  131.6 3.1 %slice-start.1 = ((s8[6291456]{0:T(1024)(128)(4,1)}), s8[2097152]{0:T(1024)(128)(4,1)S(1)}, s32[]{:S(2)}) async-start(s8[6291456]{0:T(1024)(128)(4,1)} %bitcast.197), calls=%async_computation.1 | async-start | bytes 4194304
  134.8 2.5 copy-start.30
  137.3 2.7 copy-start.6
  142.8 3.0 copy-start.34
  143.0 2.7 copy-start.36
  144.3 4.6 %copy-start.17 = (bf16[128,768]{0,1:T(8,128)(2,1)S(1)}, bf16[128,768]{0,1:T(8,128)(2,1)}, u32[]{:S(2)}) copy-start(bf16[128,768]{0,1:T(8,128)(2,1)} %copy-done.16) | copy-start | bytes 589828
  144.3 4.6 %copy-start.21 = (bf16[12,128,64]{1,2,0:T(8,128)(2,1)S(1)}, bf16[12,128,64]{1,2,0:T(8,128)(2,1)}, u32[]{:S(2)}) copy-start(bf16[12,128,64]{1,2,0:T(8,128)(2,1)} %copy-done.20) | copy-start | bytes 589828
  146.7 5.7 %copy-start.33 = (bf16[12,64,128]{2,1,0:T(8,128)(2,1)S(1)}, bf16[12,64,128]{2,1,0:T(8,128)(2,1)}, u32[]{:S(2)}) copy-start(bf16[12,64,128]{2,1,0:T(8,128)(2,1)} %copy-done.32) | copy-start | bytes 589828
  148.9 3.5 %copy-start.35 = (bf16[12,64,128]{2,1,0:T(8,128)(2,1)S(1)}, bf16[12,64,128]{2,1,0:T(8,128)(2,1)}, u32[]{:S(2)}) copy-start(bf16[12,64,128]{2,1,0:T(8,128)(2,1)} %copy-done.34) | copy-start | bytes 589828
  148.9 3.5 %copy-start.37 = (bf16[12,64,128]{2,1,0:T(8,128)(2,1)S(1)}, bf16[12,64,128]{2,1,0:T(8,128)(2,1)}, u32[]{:S(2)}) copy-start(bf16[12,64,128]{2,1,0:T(8,128)(2,1)} %copy-done.36) | copy-start | bytes 589828
  152.4 3.1 copy-start.13
  152.4 4.5 %copy-start.29 = (bf16[12,64,128]{2,1,0:T(8,128)(2,1)S(1)}, bf16[12,64,128]{2,1,0:T(8,128)(2,1)}, u32[]{:S(2)}) copy-start(bf16[12,64,128]{2,1,0:T(8,128)(2,1)} %copy-done.28) | copy-start | bytes 589828
  155.5 3.1 copy-start.38
  156.9 3.8 %copy-start.19 = (bf16[12,64,128]{2,1,0:T(8,128)(2,1)S(1)}, bf16[12,64,128]{2,1,0:T(8,128)(2,1)}, u32[]{:S(2)}) copy-start(bf16[12,64,128]{2,1,0:T(8,128)(2,1)} %copy-done.18) | copy-start | bytes 589828
  158.5 3.7 %copy-start.43 = (bf16[128,2048]{1,0:T(8,128)(2,1)S(1)}, bf16[128,2048]{1,0:T(8,128)(2,1)}, u32[]{:S(2)}) copy-start(bf16[128,2048]{1,0:T(8,128)(2,1)} %copy-done.42) | copy-start | bytes 1572868
  158.5 3.7 %copy-start.45 = (bf16[128,2048]{1,0:T(8,128)(2,1)S(1)}, bf16[128,2048]{1,0:T(8,128)(2,1)}, u32[]{:S(2)}) copy-start(bf16[128,2048]{1,0:T(8,128)(2,1)} %copy-done.44) | copy-start | bytes 1572868
  162.3 4.6 %copy-start.15 = (bf16[128,2048]{1,0:T(8,128)(2,1)S(1)}, bf16[128,2048]{1,0:T(8,128)(2,1)}, u32[]{:S(2)}) copy-start(bf16[128,2048]{1,0:T(8,128)(2,1)} %copy-done.14) | copy-start | bytes 1572868
  162.3 4.6 %copy-start.40 = (bf16[1,128,768]{2,1,0:T(8,128)(2,1)S(1)}, bf16[1,128,768]{2,1,0:T(8,128)(2,1)}, u32[]{:S(2)}) copy-start(bf16[1,128,768]{2,1,0:T(8,128)(2,1)} %param.21) | copy-start | bytes 589828
  304.7 4.7 %copy-start.46 = (f32[3,8,4096]{2,1,0:T(8,128)S(1)}, f32[3,8,4096]{2,1,0:T(8,128)}, u32[]{:S(2)}) copy-start(f32[3,8,4096]{2,1,0:T(8,128)} %get-tuple-element.38) | copy-start | bytes 1179652
  304.7 5.7 %copy-start.49 = (f32[24,128]{1,0:T(8,128)S(1)}, f32[24,128]{1,0:T(8,128)}, u32[]{:S(2)}) copy-start(f32[24,128]{1,0:T(8,128)} %get-tuple-element.40) | copy-start | bytes 36868
  304.7 7.2 %copy-start.47 = (f32[8,8,768]{2,1,0:T(8,128)S(1)}, f32[8,8,768]{2,1,0:T(8,128)}, u32[]{:S(2)}) copy-start(f32[8,8,768]{2,1,0:T(8,128)} %get-tuple-element.39) | copy-start | bytes 589828
  (23 other events, 34.5 us)

commit v2 on v0

--- a/solution.py
+++ b/solution.py
@@ -1,6 +1,10 @@
+import types
+
 import jax
 import jax.numpy as jnp
 from jax import lax
+from jax.experimental import pallas as pl
+from jax.experimental.pallas import tpu as pltpu
 from jax.sharding import PartitionSpec as P
 
 HEAD = 64
@@ -251,7 +255,7 @@
     return planes
 
 
-def per_device(
+def plain_device(
     inputs,
     encoded,
     lengths,
@@ -324,34 +328,793 @@
     )
 
 
+MESH = pl.DeviceIdType.MESH
+SUB, LANES, TILE = 8, 128, 256
+GAIN, QKV, OUT, QC, KVC, OUTC, FFIN, FFOUT = range(8)
+NT = (((1,), (1,)), ((), ()))
+TN = (((0,), (0,)), ((), ()))
+NN = (((1,), (0,)), ((), ()))
+
+
+def dot(left, right, dims=NN):
+    return lax.dot_general(left, right, dims, preferred_element_type=jnp.float32)
+
+
+def place():
+    me = lax.axis_index("fsdp")
+    return me, lax.rem(me, 2), lax.rem(me // 2, 2), lax.rem(me // 4, 2), me // 8
+
+
+def device(z, y, x, core):
+    return ((z * 2 + y) * 2 + x) * 2 + core
+
+
+def both(first, second):
+    if first is None:
+        return second
+    if second is None:
+        return first
+    return jnp.logical_and(first, second)
+
+
+def maybe(cond, action):
+    if cond is None:
+        action()
+    else:
+        pl.when(cond)(action)
+
+
+class Sender:
+    def __init__(self, sems, anyone):
+        self.sems = sems
+        self.anyone = anyone
+        self.used = 0
+        self.open = []
+
+    def start(self, src, dst, recv, target, cond=None):
+        copy = pltpu.make_async_remote_copy(
+            src_ref=src,
+            dst_ref=dst,
+            send_sem=self.sems.at[self.used],
+            recv_sem=recv,
+            device_id=(target,),
+            device_id_type=MESH,
+        )
+        self.used += 1
+        self.open.append((cond, copy))
+        maybe(cond, copy.start)
+
+    def wait(self, dst, sem, cond=None):
+        copy = pltpu.make_async_remote_copy(
+            src_ref=dst,
+            dst_ref=dst,
+            send_sem=self.sems.at[0],
+            recv_sem=sem,
+            device_id=(self.anyone,),
+            device_id_type=MESH,
+        )
+        maybe(cond, copy.wait_recv)
+
+    def finish(self):
+        for cond, copy in self.open:
+            maybe(cond, copy.wait_send)
+
+
+def chunks(total, body):
+    def step(i, carry):
+        body(i, pl.ds(pl.multiple_of(i * TILE, TILE), TILE))
+        return carry
+
+    lax.fori_loop(0, total // TILE, step, 0)
+
+
+def rms_parts(value):
+    recip = lax.rsqrt(jnp.mean(value * value, axis=-1, keepdims=True) + EPS)
+    return value * recip, recip
+
+
+def gelu_and_slope(value):
+    inner = 0.7978845608028654 * (value + 0.044715 * value * value * value)
+    bent = jnp.tanh(inner)
+    slope = 0.5 * (1.0 + bent) + 0.5 * value * (1.0 - bent * bent) * (
+        0.7978845608028654 * (1.0 + 3.0 * 0.044715 * value * value)
+    )
+    return 0.5 * value * (1.0 + bent), slope
+
+
+def layer_kernel(planes, tree, *refs):
+    r = types.SimpleNamespace(**jax.tree.unflatten(tree, refs))
+    me, core, x, y, z = place()
+    partner, across, along = device(z, y, x, 1 - core), device(z, y, 1 - x, core), device(z, 1 - y, x, core)
+    up, down = device(z + 1, y, x, core), device(z - 1, y, x, core)
+    can_up, can_down = z < planes - 1, z > 0
+    half = planes // 2
+    others = [device(lax.rem(z + k, planes), y, x, core) for k in range(1, planes)]
+    whole, shard = r.whole, r.shard
+    local_sem, recv_sem, pair_sem = r.local_sem, r.recv_sem, r.pair_sem
+    sender = Sender(r.send_sem, partner)
+
+    def load_own(g):
+        return pltpu.make_async_copy(shard[g], whole[g].at[me], local_sem.at[g])
+
+    for g in range(8):
+        load_own(g).start()
+    barrier = pltpu.get_barrier_semaphore()
+    peers = [partner, across, along, *others]
+    for peer in peers:
+        pl.semaphore_signal(barrier, inc=1, device_id=(peer,), device_id_type=MESH)
+    pl.semaphore_wait(barrier, len(peers))
+
+    def send(g, src, target, cond, own=False):
+        sender.start(
+            shard[g] if own else whole[g].at[src], whole[g].at[src], recv_sem.at[g, src], target, cond
+        )
+
+    def arrive(g, src, cond=None):
+        sender.wait(whole[g].at[src], recv_sem.at[g, src], cond)
+
+    def steps(k):
+        if k == 0:
+            return [(None, z)]
+        return [(z - k >= 0, z - k), (z + k < planes, z + k)]
+
+    def line(g, k):
+        for side, (cond, zs) in enumerate(steps(k)):
+            src = device(zs, y, x, core)
+            if k:
+                arrive(g, src, cond)
+            if k == 0 or side == 0:
+                send(g, src, up, both(cond, can_up), k == 0)
+            if k == 0 or side == 1:
+                send(g, src, down, both(cond, can_down), k == 0)
+            send(g, src, across, cond, k == 0)
+            send(g, src, along, cond, k == 0)
+            send(g, src, partner, cond, k == 0)
+
+    def plane(g, k):
+        for cond, zs in steps(k):
+            src = device(zs, y, 1 - x, core)
+            arrive(g, src, cond)
+            send(g, src, along, both(cond, zs >= half))
+            send(g, src, partner, cond)
+            src = device(zs, 1 - y, x, core)
+            arrive(g, src, cond)
+            send(g, src, across, both(cond, zs < half))
+            send(g, src, partner, cond)
+
+    def corner(g, k):
+        for cond, zs in steps(k):
+            src = device(zs, 1 - y, 1 - x, core)
+            arrive(g, src, cond)
+            send(g, src, partner, cond)
+
+    def gather_stage(g, t):
+        if t < planes:
+            line(g, t)
+        if 0 <= t - 1 < planes:
+            plane(g, t - 1)
+        if 0 <= t - 2 < planes:
+            corner(g, t - 2)
+
+    def settle(g):
+        for zs in range(planes):
+            for ys in range(2):
+                for xs in range(2):
+                    arrive(g, device(zs, ys, xs, 1 - core))
+        load_own(g).wait()
+
+    rows_t, rows_p, step_p, mine = ([None] + list(a) for a in (r.turned, r.turned_p, r.step_p, r.mine))
+    step = [None] + list(r.step) + [r.cot]
+
+    def turn(g, value):
+        shape = rows_t[g].shape
+        turned = jnp.transpose(value, (1, 0)).reshape((shape[1], 2) + shape[2:]).astype(jnp.bfloat16)
+        rows_t[g][0] = turned[:, 0]
+        rows_t[g][1] = turned[:, 1]
+
+    def send_rows(g):
+        sender.start(rows_t[g].at[1 - core], rows_p[g], pair_sem.at[g, 0], partner)
+
+    def send_step(g):
+        sender.start(step[g], step_p[g], pair_sem.at[g, 1], partner)
+
+    def weight_grad(g):
+        sender.wait(rows_p[g], pair_sem.at[g, 0])
+        sender.wait(step_p[g], pair_sem.at[g, 1])
+        tokens = rows_t[g].shape[-1]
+
+        def body(i, col):
+            left, left_p = rows_t[g][core].reshape(-1, tokens), rows_p[g][...].reshape(-1, tokens)
+            right, right_p = step[g][:, col], step_p[g][:, col]
+            if tokens % LANES == 0:
+                total = dot(
+                    jnp.concatenate([left, left_p], axis=1), jnp.concatenate([right, right_p], axis=0)
+                )
+            else:
+                total = dot(left, right) + dot(left_p, right_p)
+            mine[g][..., col] = total.reshape(mine[g].shape[:-1] + (TILE,)).astype(jnp.bfloat16)
+
+        chunks(mine[g].shape[-1], body)
+
+    from_x, from_y, line_x, line_y, line_u, line_d, own = (
+        [None] + list(a) for a in (r.from_x, r.from_y, r.line_x, r.line_y, r.line_u, r.line_d, r.own)
+    )
+    lines = (line_u, line_d)
+    half_sem, line_sem, chain_sem = r.half_sem, r.line_sem, r.chain_sem
+    low, high = pl.ds(0, half), pl.ds(half, planes - half)
+
+    def add(g, ys, xs, first, last, terms):
+        depth = mine[g].shape[3]
+
+        def body(i, carry):
+            zs, at = first + i // depth, lax.rem(i, depth)
+            total = mine[g][zs, ys, xs, at].astype(jnp.float32)
+            for term, skip in terms:
+                total = total + term[zs - skip, at].astype(jnp.float32)
+            mine[g][zs, ys, xs, at] = total.astype(jnp.bfloat16)
+            return carry
+
+        lax.fori_loop(0, (last - first) * depth, body, 0)
+
+    def scatter_stage(g, t):
+        if t == 0:
+            far = (1 - y, 1 - x)
+            sender.start(mine[g].at[(low,) + far], from_x[g], half_sem.at[g, 0], across)
+            sender.start(mine[g].at[(high,) + far], from_y[g], half_sem.at[g, 1], along)
+            sender.start(mine[g].at[low, y, 1 - x], line_x[g].at[low], line_sem.at[g, 0], across)
+            sender.start(mine[g].at[high, 1 - y, x], line_y[g].at[high], line_sem.at[g, 3], along)
+        elif t == 1:
+            sender.wait(from_y[g], half_sem.at[g, 1])
+            add(g, y, 1 - x, half, planes, [(from_y[g], half)])
+            sender.start(mine[g].at[high, y, 1 - x], line_x[g].at[high], line_sem.at[g, 1], across)
+            sender.wait(from_x[g], half_sem.at[g, 0])
+            add(g, 1 - y, x, 0, half, [(from_x[g], 0)])
+            sender.start(mine[g].at[low, 1 - y, x], line_y[g].at[low], line_sem.at[g, 2], along)
+        elif t == 2:
+            sender.wait(line_x[g].at[low], line_sem.at[g, 0])
+            sender.wait(line_x[g].at[high], line_sem.at[g, 1])
+            sender.wait(line_y[g].at[low], line_sem.at[g, 2])
+            sender.wait(line_y[g].at[high], line_sem.at[g, 3])
+            add(g, y, x, 0, planes, [(line_x[g], 0), (line_y[g], 0)])
+            chain(g, planes - 1)
+        elif t < 1 + planes:
+            chain(g, planes + 1 - t)
+        else:
+            land(g)
+
+    def chain(g, k):
+        for way, (at, inside, fed, target) in enumerate(
+            ((z + k, z + k < planes, z > 0, up), (z - k, z - k >= 0, z < planes - 1, down))
+        ):
+            spot = jnp.clip(at, 0, planes - 1)
+
+            @pl.when(both(inside, fed))
+            def _(way=way, spot=spot):
+                sender.wait(lines[way][g].at[spot], chain_sem.at[g, way, spot])
+
+                def body(at, carry):
+                    total = mine[g][spot, y, x, at].astype(jnp.float32)
+                    total = total + lines[way][g][spot, at].astype(jnp.float32)
+                    mine[g][spot, y, x, at] = total.astype(jnp.bfloat16)
+                    return carry
+
+                lax.fori_loop(0, mine[g].shape[3], body, 0)
+
+            sender.start(
+                mine[g].at[spot, y, x], lines[way][g].at[spot], chain_sem.at[g, way, spot], target, inside
+            )
+
+    def land(g):
+        sender.wait(lines[0][g].at[z], chain_sem.at[g, 0, z], can_down)
+        sender.wait(lines[1][g].at[z], chain_sem.at[g, 1, z], can_up)
+        zero = jnp.zeros(mine[g].shape[4:], jnp.float32)
+
+        def body(at, carry):
+            total = mine[g][z, y, x, at].astype(jnp.float32)
+            total = total + jnp.where(can_down, lines[0][g][z, at].astype(jnp.float32), zero)
+            total = total + jnp.where(can_up, lines[1][g][z, at].astype(jnp.float32), zero)
+            own[g][at] = total
+            return carry
+
+        lax.fori_loop(0, mine[g].shape[3], body, 0)
+
+    last_scatter = planes + 1
+
+    held, got, small_sem = r.held, r.got, r.small_sem
+
+    def small_pairs():
+        for at, peer in enumerate((partner, across, along)):
+            sender.start(held.at[at], got.at[at], small_sem.at[at], peer)
+            sender.wait(got.at[at], small_sem.at[at])
+            held[at + 1] = held[at] + got[at]
+        for peer in others:
+            sender.start(held.at[3], got.at[3 + z], small_sem.at[3 + z], peer)
+
+    def small_land():
+        for k in range(1, planes):
+            at = lax.rem(z + k, planes)
+            sender.wait(got.at[3 + at], small_sem.at[3 + at])
+        got[3 + z] = held[3]
+        total = got[3]
+        for zs in range(1, planes):
+            total = total + got[3 + zs]
+        r.small_out[...] = total
+
+    length_row, bucket_row, table = r.length, r.bucket, r.table
+    rows_in, enc, cot = r.rows, r.enc, r.cot
+    positions, width = rows_in.shape
+    pairs = width // LANES
+    hidden = r.hid.shape[1]
+    gain = r.gain
+
+    def onehot():
+        ids = lax.broadcasted_iota(jnp.int32, (table.shape[0], positions), 0)
+        return (ids == bucket_row[...]).astype(jnp.float32)
+
+    def head_lanes(which):
+        lane = lax.broadcasted_iota(jnp.int32, (1, LANES), 1) // HEAD
+        return (lane == which).astype(jnp.bfloat16)
+
+    def matmul(dst, source, g):
+        def body(i, col):
+            weight = whole[g][:, :, :, col].reshape(-1, TILE)
+            dst[:, col] = dot(source[...], weight).astype(dst.dtype)
+
+        chunks(whole[g].shape[-1], body)
+
+    def matmul_back(source, g):
+        acc = r.acc
+        count = source.shape[0]
+        acc[pl.ds(0, count), :] = jnp.zeros((count, width), jnp.float32)
+
+        def body(i, col):
+            weight = whole[g][:, :, :, col].reshape(-1, TILE)
+            acc[pl.ds(0, count), :] += dot(source[:, col], weight, NT)
+
+        chunks(whole[g].shape[-1], body)
+        return acc[pl.ds(0, count), :]
+
+    def norm_forward(value, which, dst, g):
+        normed, unused = rms_parts(value)
+        scaled = normed * gain[pl.ds(which, 1), :]
+        dst[...] = scaled.astype(jnp.bfloat16)
+        turn(g, scaled)
+        send_rows(g)
+
+    def norm_back(grad, value, which):
+        normed, recip = rms_parts(value)
+        scaled = grad * gain[pl.ds(which, 1), :]
+        held[0, pl.ds(which, 1), :] = jnp.sum(grad * normed, axis=0, keepdims=True)
+        return recip * (scaled - normed * jnp.mean(scaled * normed, axis=-1, keepdims=True))
+
+    def per_pair(body):
+        def run(j, carry):
+            body(j, lambda base: pl.ds(pl.multiple_of(base + j * LANES, LANES), LANES))
+            return carry
+
+        lax.fori_loop(0, pairs, run, 0)
+
+    def start_compute():
+        gain[...] = jnp.sum(whole[GAIN][...].astype(jnp.float32), axis=(0, 1))
+        spread = lax.dot_general(
+            table[...], onehot(), TN, precision=lax.Precision.HIGHEST, preferred_element_type=jnp.float32
+        )
+        r.by_dist[pl.ds(0, spread.shape[0]), :] = spread
+        norm_forward(rows_in[...].astype(jnp.float32), 0, r.h1, QKV)
+
+    def early():
+        turn(KVC, enc[...].astype(jnp.float32))
+        send_rows(KVC)
+        send_step(FFOUT)
+
+    def self_attention():
+        matmul(r.qkv, r.h1, QKV)
+        row_ids = lax.broadcasted_iota(jnp.int32, (positions, positions), 0)
+        col_ids = lax.broadcasted_iota(jnp.int32, (positions, positions), 1)
+        qkv = r.qkv
+
+        def body(j, at):
+            live = (col_ids <= row_ids) & (col_ids < length_row[...])
+            query, key, value = qkv[:, at(0)], qkv[:, at(width)], qkv[:, at(2 * width)]
+            out = jnp.zeros((positions, LANES), jnp.float32)
+            for e in range(2):
+                lanes = head_lanes(e)
+                head = 2 * j + e
+                bias = jnp.broadcast_to(r.by_dist[pl.ds(head, 1), :], (positions, positions))
+                bias = pltpu.roll(bias, 0, 1, stride=1, stride_axis=0)
+                scores = jnp.where(live, dot(query * lanes, key, NT) + bias, -1e30)
+                top = jnp.max(scores, axis=-1, keepdims=True)
+                lse = top + jnp.log(jnp.sum(jnp.exp(scores - top), axis=-1, keepdims=True))
+                prob = jnp.exp(scores - lse)
+                r.prob[head] = prob
+                out = out + dot(prob.astype(jnp.bfloat16), value * lanes)
+            r.att[:, at(0)] = out.astype(jnp.bfloat16)
+
+        per_pair(body)
+        turn(OUT, r.att[...].astype(jnp.float32))
+        send_rows(OUT)
+
+    def after_self():
+        def body(i, col):
+            weight = whole[OUT][:, :, :, col].reshape(-1, TILE)
+            r.x1[:, col] = rows_in[:, col].astype(jnp.float32) + dot(r.att[...], weight)
+
+        chunks(width, body)
+        norm_forward(r.x1[...], 1, r.h2, QC)
+
+    def cross_attention():
+        matmul(r.kvc, enc, KVC)
+        kvc = r.kvc
+
+        def body(j, at):
+            query, key, value = r.qc[:, at(0)], kvc[:, at(0)], kvc[:, at(width)]
+            out = jnp.zeros((positions, LANES), jnp.float32)
+            for e in range(2):
+                lanes = head_lanes(e)
+                scores = dot(query * lanes, key, NT)
+                lse = jnp.log(jnp.sum(jnp.exp(scores), axis=-1, keepdims=True))
+                prob = jnp.exp(scores - lse)
+                r.prob_c[2 * j + e] = prob
+                out = out + dot(prob.astype(jnp.bfloat16), value * lanes)
+            r.att_c[:, at(0)] = out.astype(jnp.bfloat16)
+
+        per_pair(body)
+        turn(OUTC, r.att_c[...].astype(jnp.float32))
+        send_rows(OUTC)
+
+    def after_cross():
+        def body(i, col):
+            weight = whole[OUTC][:, :, :, col].reshape(-1, TILE)
+            r.x2[:, col] = r.x1[:, col] + dot(r.att_c[...], weight)
+
+        chunks(width, body)
+        norm_forward(r.x2[...], 2, r.h3, FFIN)
+
+    def feed():
+        gate_up = r.gate_up
+        matmul(gate_up, r.h3, FFIN)
+        turned = rows_t[FFOUT]
+        tall = turned.shape[2] * turned.shape[3]
+        chips = TILE // (2 * tall)
+
+        def body(i, col):
+            up_col = pl.ds(pl.multiple_of(hidden + i * TILE, TILE), TILE)
+            value, unused = gelu_and_slope(gate_up[:, col])
+            product = value * gate_up[:, up_col]
+            r.hid[:, col] = product.astype(jnp.bfloat16)
+            flipped = jnp.transpose(product, (1, 0)).reshape((chips, 2) + turned.shape[2:])
+            flipped = flipped.astype(jnp.bfloat16)
+            turned[0, pl.ds(i * chips, chips)] = flipped[:, 0]
+            turned[1, pl.ds(i * chips, chips)] = flipped[:, 1]
+
+        chunks(hidden, body)
+        send_rows(FFOUT)
+
+    def feed_back():
+        gate_up, change = r.gate_up, step[FFIN]
+        tall = whole[FFOUT].shape[1] * SUB
+        devices = TILE // tall
+
+        def body(i, col):
+            up_col = pl.ds(pl.multiple_of(hidden + i * TILE, TILE), TILE)
+            weight = whole[FFOUT][pl.ds(i * devices, devices)].reshape(TILE, width)
+            d_hidden = dot(cot[...], weight, NT)
+            value, slope = gelu_and_slope(gate_up[:, col])
+            change[:, col] = (d_hidden * gate_up[:, up_col] * slope).astype(jnp.bfloat16)
+            change[:, up_col] = (d_hidden * value).astype(jnp.bfloat16)
+
+        chunks(hidden, body)
+        send_step(FFIN)
+
+    def finish_forward():
+        def body(i, col):
+            weight = whole[FFOUT][:, :, :, col].reshape(-1, TILE)
+            r.result[:, col] = (r.x2[:, col] + dot(r.hid[...], weight)).astype(jnp.bfloat16)
+
+        chunks(width, body)
+
+    def before_cross():
+        back = norm_back(matmul_back(step[FFIN], FFIN), r.x2[...], 2)
+        r.dx[...] = cot[...].astype(jnp.float32) + back
+        step[OUTC][...] = r.dx[...].astype(jnp.bfloat16)
+        send_step(OUTC)
+
+    def cross_attention_back():
+        d_att = matmul_back_rows(step[OUTC], OUTC)
+        kvc = r.kvc
+
+        def body(j, at):
+            query, key, value = r.qc[:, at(0)], kvc[:, at(0)], kvc[:, at(width)]
+            grad, out = d_att[:, at(0)], r.att_c[:, at(0)].astype(jnp.float32)
+            grads = attend_pair_back(j, query, key, value, grad, out, r.prob_c, None)
+            step[QC][:, at(0)] = grads[0].astype(jnp.bfloat16)
+            step[KVC][:, at(0)] = grads[1].astype(jnp.bfloat16)
+            step[KVC][:, at(width)] = grads[2].astype(jnp.bfloat16)
+
+        per_pair(body)
+        send_step(KVC)
+        send_step(QC)
+
+    def matmul_back_rows(source, g):
+        r.d_att[...] = matmul_back(source, g)
+        return r.d_att
+
+    def attend_pair_back(j, query, key, value, grad, out, probs, spread):
+        grad_b = grad.astype(jnp.bfloat16)
+        d_query, d_key, d_value = 0.0, 0.0, 0.0
+        for e in range(2):
+            lanes = head_lanes(e)
+            prob = probs[2 * j + e]
+            inside = lax.broadcasted_iota(jnp.int32, (positions, LANES), 1) // HEAD == e
+            delta = jnp.sum(jnp.where(inside, grad * out, 0.0), axis=-1, keepdims=True)
+            d_prob = dot(grad_b * lanes, value, NT)
+            d_score = prob * (d_prob - delta)
+            if spread is not None:
+                spread(2 * j + e, d_score)
+            d_score_b = d_score.astype(jnp.bfloat16)
+            d_value = d_value + dot(prob.astype(jnp.bfloat16), grad_b * lanes, TN)
+            d_query = d_query + dot(d_score_b, key * lanes)
+            d_key = d_key + dot(d_score_b, query * lanes, TN)
+        return d_query, d_key, d_value
+
+    def between():
+        r.enc_grad[...] = matmul_back(step[KVC], KVC).astype(jnp.bfloat16)
+        back = norm_back(matmul_back(step[QC], QC), r.x1[...], 1)
+        r.dx[...] += back
+        step[OUT][...] = r.dx[...].astype(jnp.bfloat16)
+        send_step(OUT)
+
+    def self_attention_back():
+        d_att = matmul_back_rows(step[OUT], OUT)
+        qkv = r.qkv
+        row = lax.broadcasted_iota(jnp.int32, (SUB, positions), 0)
+
+        def spread(head, d_score):
+            total, count = d_score, positions // 2
+            while count >= SUB:
+                total = total[:count] + pltpu.roll(total[count:], positions - count, 1)
+                count //= 2
+            for bit in (4, 2, 1):
+                total = jnp.where(
+                    lax.rem(row // bit, 2) == 1, pltpu.roll(total, positions - bit, 1), total
+                )
+            r.by_dist[pl.ds(head, 1), :] = jnp.sum(total, axis=0, keepdims=True)
+
+        def body(j, at):
+            query, key, value = qkv[:, at(0)], qkv[:, at(width)], qkv[:, at(2 * width)]
+            grad, out = d_att[:, at(0)], r.att[:, at(0)].astype(jnp.float32)
+            grads = attend_pair_back(j, query, key, value, grad, out, r.prob, spread)
+            for part in range(3):
+                step[QKV][:, at(part * width)] = grads[part].astype(jnp.bfloat16)
+
+        per_pair(body)
+        send_step(QKV)
+
+    def last():
+        back = norm_back(matmul_back(step[QKV], QKV), rows_in[...].astype(jnp.float32), 0)
+        r.input_grad[...] = (r.dx[...] + back).astype(jnp.bfloat16)
+        sums = lax.dot_general(
+            r.by_dist[...], onehot(), NT, precision=lax.Precision.HIGHEST,
+            preferred_element_type=jnp.float32,
+        )
+        held[0, pl.ds(SUB, sums.shape[0]), pl.ds(0, sums.shape[1])] = sums
+
+    held[0] = jnp.zeros(held.shape[1:], jnp.float32)
+    r.by_dist[...] = jnp.zeros(r.by_dist.shape, jnp.float32)
+    gathers = {GAIN: 0, QKV: 0, OUT: 2, QC: 2, KVC: 3, OUTC: 4, FFIN: 5, FFOUT: 7}
+    ready = {
+        GAIN: start_compute,
+        QKV: self_attention,
+        OUT: after_self,
+        QC: lambda: matmul(r.qc, r.h2, QC),
+        KVC: cross_attention,
+        OUTC: after_cross,
+        FFIN: feed,
+    }
+    for now in range(max(gathers.values()) + planes + 2):
+        for g, begin in gathers.items():
+            if 0 <= now - begin < planes + 2:
+                gather_stage(g, now - begin)
+        if now == 0:
+            early()
+        for g, begin in gathers.items():
+            if now - begin == planes + 1 and g != FFOUT:
+                settle(g)
+                ready[g]()
+    weight_grad(FFOUT)
+    settle(FFOUT)
+    slots = [
+        (feed_back, FFOUT),
+        (before_cross, None),
+        (lambda: weight_grad(FFIN), FFIN),
+        (finish_forward, None),
+        (cross_attention_back, None),
+        (lambda: weight_grad(OUTC), OUTC),
+        (between, None),
+        (lambda: (weight_grad(KVC), weight_grad(QC)), (KVC, QC)),
+        (self_attention_back, None),
+        (lambda: weight_grad(OUT), OUT),
+        (last, None),
+        (lambda: weight_grad(QKV), QKV),
+        (small_pairs, None),
+    ]
+    begun = {FFOUT: 0}
+    scatter_stage(FFOUT, 0)
+    now = 0
+    while now < len(slots) or any(now - b <= last_scatter for b in begun.values()):
+        if now < len(slots):
+            work, groups = slots[now]
+            work()
+            if groups is not None and groups != FFOUT:
+                for g in groups if isinstance(groups, tuple) else (groups,):
+                    begun[g] = now
+                    scatter_stage(g, 0)
+        for g, begin in begun.items():
+            if 1 <= now - begin <= last_scatter:
+                scatter_stage(g, now - begin)
+        now += 1
+    small_land()
+    sender.finish()
+
+
+def per_device(
+    inputs, encoded, lengths, bucket_ids, qkv_weights, out_weights, ff_in, ff_out, gains, bias_table, cotangent
+):
+    count = lax.axis_size("fsdp")
+    me = lax.axis_index("fsdp")
+    planes = count // 8
+    half = planes // 2
+    depth, width, hidden = qkv_weights.shape[0], qkv_weights.shape[-1], ff_in.shape[-1]
+    positions, keys = inputs.shape[1], encoded.shape[1]
+    heads, buckets = bias_table.shape[1], bias_table.shape[0]
+    gain_row = lax.dynamic_update_slice(
+        jnp.zeros((SUB, width), jnp.bfloat16), gains, (jnp.int32(0), me * gains.shape[1])
+    )
+    shards = [
+        gain_row,
+        qkv_weights[:, 0:3].reshape(depth, 3 * width),
+        out_weights[:, 0],
+        qkv_weights[:, 3],
+        qkv_weights[:, 4:6].reshape(depth, 2 * width),
+        out_weights[:, 1],
+        ff_in.reshape(depth, 2 * hidden),
+        ff_out,
+    ]
+    shards = [s.reshape(-1, SUB, s.shape[-1]) for s in shards]
+    backward_ids = jnp.concatenate([bucket_ids[:1], bucket_ids[:0:-1]])[None]
+    length_row = jnp.broadcast_to(lengths[:, None], (1, positions))
+    bf, fl = jnp.bfloat16, jnp.float32
+    any_spec, vmem = pl.BlockSpec(memory_space=pl.ANY), pl.BlockSpec(memory_space=pltpu.VMEM)
+    ins = dict(
+        shard=shards,
+        rows=inputs[0],
+        enc=encoded[0],
+        cot=cotangent[0],
+        length=length_row,
+        bucket=backward_ids,
+        table=bias_table,
+    )
+    in_specs = [any_spec if s.ndim == 3 else vmem for s in jax.tree.leaves(ins)]
+    padded = 2 * SUB * -(-heads // (2 * SUB))
+    small = (SUB + padded, width)
+    square = (positions, width)
+    kinds = range(1, 8)
+    shape = jax.ShapeDtypeStruct
+    outs = dict(
+        result=shape(square, bf),
+        input_grad=shape(square, bf),
+        enc_grad=shape((keys, width), bf),
+        small_out=shape(small, fl),
+        own=[shape(shards[g].shape, fl) for g in kinds],
+    )
+    room, sems = pltpu.VMEM, pltpu.SemaphoreType.DMA
+    tokens = [keys if g == KVC else positions for g in range(8)]
+    blocks = [s.shape for s in shards]
+    chips = count // 2
+
+    def rows_room(lead, g):
+        return room(lead + (chips, blocks[g][0], SUB, tokens[g]), bf)
+
+    def block_rooms(*lead):
+        return [room(lead + blocks[g], bf) for g in kinds]
+
+    rooms = dict(
+        whole=[room((count,) + b, bf) for b in blocks],
+        turned=[rows_room((2,), g) for g in kinds],
+        turned_p=[rows_room((), g) for g in kinds],
+        step=[room((tokens[g], blocks[g][2]), bf) for g in kinds if g != FFOUT],
+        step_p=[room((tokens[g], blocks[g][2]), bf) for g in kinds],
+        mine=block_rooms(planes, 2, 2),
+        from_x=block_rooms(half),
+        from_y=block_rooms(planes - half),
+        line_x=block_rooms(planes),
+        line_y=block_rooms(planes),
+        line_u=block_rooms(planes),
+        line_d=block_rooms(planes),
+        gain=room((SUB, width), fl),
+        by_dist=room((padded, positions), fl),
+        h1=room(square, bf),
+        h2=room(square, bf),
+        h3=room(square, bf),
+        qkv=room((positions, 3 * width), bf),
+        qc=room(square, bf),
+        kvc=room((keys, 2 * width), bf),
+        att=room(square, bf),
+        att_c=room(square, bf),
+        prob=room((heads, positions, positions), fl),
+        prob_c=room((heads, positions, keys), fl),
+        x1=room(square, fl),
+        x2=room(square, fl),
+        dx=room(square, fl),
+        acc=room(square, fl),
+        d_att=room(square, fl),
+        gate_up=room((positions, 2 * hidden), fl),
+        hid=room((positions, hidden), bf),
+        held=room((4,) + small, fl),
+        got=room((3 + planes,) + small, fl),
+        local_sem=sems((8,)),
+        send_sem=sems((8 * (10 * planes + 8 * planes - 8) + 7 * (4 + 2 * planes) + 16 + planes,)),
+        recv_sem=sems((8, count)),
+        pair_sem=sems((8, 2)),
+        half_sem=sems((8, 2)),
+        line_sem=sems((8, 4)),
+        chain_sem=sems((8, 2, planes)),
+        small_sem=sems((3 + planes,)),
+    )
+
+    in_leaves, out_leaves, room_leaves = jax.tree.leaves(ins), jax.tree.leaves(outs), jax.tree.leaves(rooms)
+    sizes = [len(in_leaves), len(out_leaves), len(room_leaves)]
+    at = iter(range(sum(sizes)))
+    order = {}
+    for part in (ins, outs, rooms):
+        order.update(jax.tree.map(lambda unused: next(at), part))
+    numbers, tree = jax.tree.flatten(order)
+    done = pl.pallas_call(
+        lambda *refs: layer_kernel(planes, tree, *[refs[i] for i in numbers]),
+        out_shape=out_leaves,
+        in_specs=in_specs,
+        out_specs=[vmem] * len(out_leaves),
+        scratch_shapes=room_leaves,
+        compiler_params=pltpu.CompilerParams(
+            collective_id=0, has_side_effects=True, vmem_limit_bytes=62 * 1024 * 1024
+        ),
+        name="layer",
+    )(*in_leaves)
+    done = types.SimpleNamespace(**jax.tree.unflatten(jax.tree.structure(outs), done))
+    result, dx, enc_grad, total = done.result, done.input_grad, done.enc_grad, done.small_out
+    done = done.own
+    o_qkv, o_o, o_qc, o_kvc, o_oc, o_in, o_out = (o.reshape(-1, o.shape[-1]) for o in done)
+    s_gain = lax.dynamic_slice(
+        total[: gains.shape[0]], (jnp.int32(0), me * gains.shape[1]), gains.shape
+    )
+    s_table = jnp.transpose(total[SUB : SUB + heads, :buckets])
+    return (
+        result[None],
+        dx[None],
+        enc_grad[None],
+        jnp.concatenate([o_qkv, o_qc, o_kvc], axis=1).reshape(qkv_weights.shape),
+        jnp.concatenate([o_o, o_oc], axis=1).reshape(out_weights.shape),
+        o_in.reshape(ff_in.shape),
+        o_out,
+        s_gain,
+        s_table,
+    )
+
+
 def solution(mesh):
-    placed = (
-        P("fsdp", None, None),
-        P("fsdp", None, None),
-        P("fsdp"),
-        P(),
-        P("fsdp", None, None),
-        P("fsdp", None, None),
-        P("fsdp", None, None),
-        P("fsdp", None),
-        P(None, "fsdp"),
-        P(),
-        P("fsdp", None, None),
-    )
+    count = mesh.shape["fsdp"]
+
+    def layer(*args):
+        depth, tall = args[4].shape[0], args[7].shape[0]
+        tiled = depth % SUB == 0 and tall % SUB == 0 and count % 8 == 0 and count > 8
+        tiled = tiled and TILE % (2 * tall) == 0 and args[0].shape[1] == LANES and LANES == 2 * HEAD
+        return (per_device if tiled else plain_device)(*args)
+
+    rows, split = P("fsdp", None, None), P("fsdp", None)
     return jax.shard_map(
-        per_device,
+        layer,
         mesh=mesh,
-        in_specs=placed,
-        out_specs=(
-            P("fsdp", None, None),
-            P("fsdp", None, None),
-            P("fsdp", None, None),
-            P("fsdp", None, None),
-            P("fsdp", None, None),
-            P("fsdp", None, None),
-            P("fsdp", None),
-            P(None, "fsdp"),
-            P(),
-        ),
+        in_specs=(rows, rows, P("fsdp"), P(), rows, rows, rows, split, P(None, "fsdp"), P(), rows),
+        out_specs=(rows, rows, rows, rows, rows, rows, split, P(None, "fsdp"), P()),
         check_vma=False,
     )

time: 538 us -> 235 us (0.44)
  waiting for transfers between devices: 290 us -> 0 us
  Pallas kernels: 0 us -> 212 us
  local copies, waits for them, and re-layouts: 134 us -> 19.8 us
  matrix products: 47.5 us -> 0 us
  blocking collectives: 38.4 us -> 0 us
  between operations: 15.8 us -> 1.39 us
  other arithmetic: 10 us -> 1.45 us
    pallas_call x0 -> x1, Pallas kernels: none -> 212 us  [per_device(): pl.pallas_call(lambda *refs: layer_kernel(planes, tree, *[refs[i] for i i...]
    reduce_scatter x1 -> x0, waiting for transfers between devices: 167 us -> none  [per_device(): lax.psum_scatter(send, 'fsdp', scatter_dimension=0, tiled=False)]
    all_gather x1 -> x0, waiting for transfers between devices: 123 us -> none  [per_device(): whole = lax.all_gather(packed, 'fsdp', axis=0, tiled=False)]
    dot_general x35 -> x0, matrix products: 47.5 us -> none  [the longest x33 45.6 us: prod(): return jnp.einsum(form, left, right, preferred_element_type=jnp.float32)]
    psum x1 -> x0, blocking collectives: 38.4 us -> none  [per_device(): s_table = lax.psum(g_table, 'fsdp')]
    unnamed x174 -> x33, local copies, waits for them, and re-layouts: 36.2 us -> 6.14 us
    slice x30 -> x9, local copies, waits for them, and re-layouts: 30.3 us -> 2.81 us  [the longest x3 0.95 us: per_device(): qkv_weights[:, 0:3].reshape(depth, 3 * width)]
    optimization_barrier x1 -> x0, local copies, waits for them, and re-layouts: 22.3 us -> none  [per_device(): stacked, ff_out_all = lax.optimization_barrier((stacked, ff_out_all))]
  transfers between devices with their start and end apart: 2 -> 0, of which waited for: 2 -> 0; matrix products, arithmetic and copies ran while one was open for 3% -> 0% of each run, Pallas kernels for 0% -> 0%
where the time goes in v2:
time: 235 us; the launch traced here: 234 us
  Pallas kernels  212 us (90%)
  local copies, waits for them, and re-layouts  19.8 us (8%)
    pallas_call x1, Pallas kernels, per_device(): pl.pallas_call(lambda *refs: layer_kernel(planes, tree, *[refs[i] for i i...  212 us
    unnamed x33, local copies, waits for them, and re-layouts  6.14 us

profile of v2, /device:TPU:0, one launch (start us, length us, event | category | flops | bytes accessed | tf_op | source)
XLA Modules:
  0.0 234.5 jit_solution(12620664771253554935)
XLA Ops:
  1.3 0.5 broadcast_in_dim.25.refs_3_
  1.8 0.7 copy-done.13
  2.6 0.6 add_bitcast_fusion.refs_0_
  3.3 0.7 copy-done.12
  3.9 0.2 dynamic_update_slice.4.refs_5_
  4.2 0.7 copy.29.refs_13_
  4.8 1.4 slice_bitcast_fusion.refs_8_
  6.2 0.9 slice-done
  7.2 0.7 reshape_reshape.13.refs_9_
  7.9 0.9 slice-done.1
  8.8 0.8 reshape_reshape.12.refs_6_
  9.7 0.1 fusion
  9.8 0.6 copy_bitcast_fusion.1
  10.5 0.2 copy-done.3
  10.6 0.8 reshape_reshape.14.refs_11_
  11.4 211.8 %layer.1 = (bf16[64,768]{1,0:T(8,128)(2,1)}, bf16[128,768]{1,0:T(8,128)(2,1)}, f32[3,8,2304]{2,1,0:T(8,128)}, f32[3,8,768]{2,1,0:T(8,128)}, f32[3,8,768]{2,1,0:T...) custom-call(s32[1,128]{1,0:T(1,128)} %add_bitcast_fusion.refs_0_, ...), custom_call_target="tpu_custom_call" | custom-call | tf_op jit(solution)/shard_map/layer/pallas_call | solution.py:1072
  223.2 1.3 slice_bitcast_fusion.1
  224.6 0.7 slice.34
  225.3 0.6 constant_dynamic-slice_fusion
  226.0 1.0 copy.30
  226.9 1.0 copy.31
  227.9 0.8 pad_maximum_fusion.1
  228.7 1.1 reshape_reshape.15
  229.8 0.8 copy.39
  230.6 0.2 copy-done.6
  230.9 0.7 copy.46
  231.5 0.3 copy-done.5
  231.8 0.7 copy.47
  232.5 0.3 copy-done.8
  232.8 0.6 copy.48
  233.5 0.3 copy-done.4
  233.8 0.7 copy.49
  (29 shorter events, 0.5 us)
Async XLA Ops:
  1.8 0.7 copy-start.13
  3.2 0.7 copy-start.12
  3.3 0.9 copy-start.11
  4.1 0.7 copy-start.10
  6.2 0.9 slice-start
  7.9 0.9 slice-start.1
  8.8 0.9 copy-start.1
  9.7 0.9 copy-start.3
  223.2 5.5 %copy-start = (f32[3,8,4096]{2,1,0:T(8,128)S(1)}, f32[3,8,4096]{2,1,0:T(8,128)}, u32[]{:S(2)}) copy-start(f32[3,8,4096]{2,1,0:T(8,128)} %get-tuple-element.28) | copy-start | bytes 1179652
  228.7 1.1 copy-start.2
  228.7 1.1 copy-start.7
  228.7 1.1 copy-start.9
  229.8 1.0 copy-start.6
  230.8 1.0 copy-start.5
  231.8 1.0 copy-start.8
  232.8 1.0 copy-start.4

commit v3 on v2

--- a/solution.py
+++ b/solution.py
@@ -430,8 +430,31 @@
     can_up, can_down = z < planes - 1, z > 0
     half = planes // 2
     others = [device(lax.rem(z + k, planes), y, x, core) for k in range(1, planes)]
-    whole, shard = r.whole, r.shard
-    local_sem, recv_sem, pair_sem = r.local_sem, r.recv_sem, r.pair_sem
+    whole = r.whole
+    wide = r.rows.shape[1]
+    gain_in, qkv_in, out_in, ff_in, ff_out = r.shard
+    shard = [
+        gain_in,
+        qkv_in.at[:, :, pl.ds(0, 3 * wide)],
+        out_in.at[:, :, pl.ds(0, wide)],
+        qkv_in.at[:, :, pl.ds(3 * wide, wide)],
+        qkv_in.at[:, :, pl.ds(4 * wide, 2 * wide)],
+        out_in.at[:, :, pl.ds(wide, wide)],
+        ff_in,
+        ff_out,
+    ]
+    qkv_own, out_own, in_own, down_own = r.own
+    own = [
+        None,
+        (qkv_own, 0),
+        (out_own, 0),
+        (qkv_own, 3 * wide),
+        (qkv_own, 4 * wide),
+        (out_own, wide),
+        (in_own, 0),
+        (down_own, 0),
+    ]
+    local_sem, recv_sem, pair_sem, share_sem = r.local_sem, r.recv_sem, r.pair_sem, r.share_sem
     sender = Sender(r.send_sem, partner)
 
     def load_own(g):
@@ -471,21 +494,49 @@
             send(g, src, along, cond, k == 0)
             send(g, src, partner, cond, k == 0)
 
+    def shares(g):
+        deep = whole[g].shape[1]
+        by_line = deep // 3
+        return (0, deep - 2 * by_line), (deep - 2 * by_line, by_line), (deep - by_line, by_line)
+
+    def send_share(g, src, which, sem, target, cond):
+        first, number = shares(g)[which]
+        if number:
+            part = whole[g].at[src, pl.ds(first, number)]
+            sender.start(part, part, sem, target, cond)
+
+    def arrive_share(g, src, which, sem, cond):
+        first, number = shares(g)[which]
+        if number:
+            sender.wait(whole[g].at[src, pl.ds(first, number)], sem, cond)
+
     def plane(g, k):
         for cond, zs in steps(k):
             src = device(zs, y, 1 - x, core)
             arrive(g, src, cond)
-            send(g, src, along, both(cond, zs >= half))
+            send_share(g, src, 0, recv_sem.at[g, src], along, both(cond, zs >= half))
+            if k == 0:
+                send_share(g, src, 2, share_sem.at[g, 1, z], along, cond)
             send(g, src, partner, cond)
             src = device(zs, 1 - y, x, core)
             arrive(g, src, cond)
-            send(g, src, across, both(cond, zs < half))
+            send_share(g, src, 0, recv_sem.at[g, src], across, both(cond, zs < half))
+            if k == 0:
+                send_share(g, src, 1, share_sem.at[g, 0, z], across, cond)
             send(g, src, partner, cond)
 
     def corner(g, k):
-        for cond, zs in steps(k):
+        for side, (cond, zs) in enumerate(steps(k)):
             src = device(zs, 1 - y, 1 - x, core)
-            arrive(g, src, cond)
+            spot = zs if cond is None else jnp.clip(zs, 0, planes - 1)
+            for way in range(2):
+                sem = share_sem.at[g, way, spot]
+                arrive_share(g, src, way + 1, sem, cond)
+                if k == 0 or side == 0:
+                    send_share(g, src, way + 1, sem, up, both(cond, can_up))
+                if k == 0 or side == 1:
+                    send_share(g, src, way + 1, sem, down, both(cond, can_down))
+            arrive_share(g, src, 0, recv_sem.at[g, src], cond)
             send(g, src, partner, cond)
 
     def gather_stage(g, t):
@@ -536,8 +587,8 @@
 
         chunks(mine[g].shape[-1], body)
 
-    from_x, from_y, line_x, line_y, line_u, line_d, own = (
-        [None] + list(a) for a in (r.from_x, r.from_y, r.line_x, r.line_y, r.line_u, r.line_d, r.own)
+    from_x, from_y, line_x, line_y, line_u, line_d = (
+        [None] + list(a) for a in (r.from_x, r.from_y, r.line_x, r.line_y, r.line_u, r.line_d)
     )
     lines = (line_u, line_d)
     half_sem, line_sem, chain_sem = r.half_sem, r.line_sem, r.chain_sem
@@ -577,8 +628,12 @@
             sender.wait(line_y[g].at[high], line_sem.at[g, 3])
             add(g, y, x, 0, planes, [(line_x[g], 0), (line_y[g], 0)])
             chain(g, planes - 1)
-        elif t < 1 + planes:
-            chain(g, planes + 1 - t)
+        elif t == 3:
+            for k in range(planes - 2, 1, -1):
+                chain(g, k)
+        elif t == 4:
+            if planes > 2:
+                chain(g, 1)
         else:
             land(g)
 
@@ -613,12 +668,11 @@
             total = mine[g][z, y, x, at].astype(jnp.float32)
             total = total + jnp.where(can_down, lines[0][g][z, at].astype(jnp.float32), zero)
             total = total + jnp.where(can_up, lines[1][g][z, at].astype(jnp.float32), zero)
-            own[g][at] = total
+            target, first = own[g]
+            target[at, :, pl.ds(first, total.shape[1])] = total
             return carry
 
         lax.fori_loop(0, mine[g].shape[3], body, 0)
-
-    last_scatter = planes + 1
 
     held, got, small_sem = r.held, r.got, r.small_sem
 
@@ -938,21 +992,38 @@
         (lambda: weight_grad(QKV), QKV),
         (small_pairs, None),
     ]
-    begun = {FFOUT: 0}
+    after = {
+        1: [(FFOUT, 1)],
+        3: [(FFOUT, 2)],
+        5: [(FFOUT, 3)],
+        6: [(FFIN, 1), (FFOUT, 4)],
+        8: [(OUTC, 1), (FFOUT, 5)],
+        10: [(FFIN, 2)],
+        11: [(KVC, 1), (QC, 1)],
+    }
+    tail = [
+        [(OUTC, 2), (FFIN, 3)],
+        [(OUT, 1), (QKV, 1), (OUTC, 3), (FFIN, 4)],
+        [(KVC, 2), (QC, 2), (OUTC, 4), (FFIN, 5)],
+        [(OUT, 2), (KVC, 3), (QC, 3), (OUTC, 5)],
+        [(QKV, 2), (OUT, 3), (KVC, 4), (QC, 4)],
+        [(QKV, 3), (OUT, 4), (KVC, 5), (QC, 5)],
+        [(QKV, 4), (OUT, 5)],
+        [(QKV, 5)],
+    ]
+    def scatter_steps(batch):
+        for g, t in batch:
+            scatter_stage(g, t)
+
     scatter_stage(FFOUT, 0)
-    now = 0
-    while now < len(slots) or any(now - b <= last_scatter for b in begun.values()):
-        if now < len(slots):
-            work, groups = slots[now]
-            work()
-            if groups is not None and groups != FFOUT:
-                for g in groups if isinstance(groups, tuple) else (groups,):
-                    begun[g] = now
-                    scatter_stage(g, 0)
-        for g, begin in begun.items():
-            if 1 <= now - begin <= last_scatter:
-                scatter_stage(g, now - begin)
-        now += 1
+    for now, (work, groups) in enumerate(slots):
+        work()
+        if groups is not None and groups != FFOUT:
+            for g in groups if isinstance(groups, tuple) else (groups,):
+                scatter_stage(g, 0)
+        scatter_steps(after.get(now, []))
+    for batch in tail:
+        scatter_steps(batch)
     small_land()
     sender.finish()
 
@@ -972,15 +1043,16 @@
     )
     shards = [
         gain_row,
-        qkv_weights[:, 0:3].reshape(depth, 3 * width),
-        out_weights[:, 0],
-        qkv_weights[:, 3],
-        qkv_weights[:, 4:6].reshape(depth, 2 * width),
-        out_weights[:, 1],
+        qkv_weights.reshape(depth, 6 * width),
+        out_weights.reshape(depth, 2 * width),
         ff_in.reshape(depth, 2 * hidden),
         ff_out,
     ]
     shards = [s.reshape(-1, SUB, s.shape[-1]) for s in shards]
+    deep, tall = depth // SUB, ff_out.shape[0] // SUB
+    widths = [width, 3 * width, width, width, 2 * width, width, 2 * hidden, width]
+    deeps = [1] + [deep] * 6 + [tall]
+    blocks = [(d, SUB, w) for d, w in zip(deeps, widths)]
     backward_ids = jnp.concatenate([bucket_ids[:1], bucket_ids[:0:-1]])[None]
     length_row = jnp.broadcast_to(lengths[:, None], (1, positions))
     bf, fl = jnp.bfloat16, jnp.float32
@@ -1005,11 +1077,10 @@
         input_grad=shape(square, bf),
         enc_grad=shape((keys, width), bf),
         small_out=shape(small, fl),
-        own=[shape(shards[g].shape, fl) for g in kinds],
+        own=[shape(s.shape, fl) for s in shards[1:]],
     )
     room, sems = pltpu.VMEM, pltpu.SemaphoreType.DMA
     tokens = [keys if g == KVC else positions for g in range(8)]
-    blocks = [s.shape for s in shards]
     chips = count // 2
 
     def rows_room(lead, g):
@@ -1053,9 +1124,10 @@
         held=room((4,) + small, fl),
         got=room((3 + planes,) + small, fl),
         local_sem=sems((8,)),
-        send_sem=sems((8 * (10 * planes + 8 * planes - 8) + 7 * (4 + 2 * planes) + 16 + planes,)),
+        send_sem=sems((8 * (24 * planes) + 7 * (4 + 2 * planes) + 16 + planes,)),
         recv_sem=sems((8, count)),
         pair_sem=sems((8, 2)),
+        share_sem=sems((8, 2, planes)),
         half_sem=sems((8, 2)),
         line_sem=sems((8, 4)),
         chain_sem=sems((8, 2, planes)),
@@ -1083,7 +1155,7 @@
     done = types.SimpleNamespace(**jax.tree.unflatten(jax.tree.structure(outs), done))
     result, dx, enc_grad, total = done.result, done.input_grad, done.enc_grad, done.small_out
     done = done.own
-    o_qkv, o_o, o_qc, o_kvc, o_oc, o_in, o_out = (o.reshape(-1, o.shape[-1]) for o in done)
+    o_qkv, o_out, o_in, o_down = (o.reshape(-1, o.shape[-1]) for o in done)
     s_gain = lax.dynamic_slice(
         total[: gains.shape[0]], (jnp.int32(0), me * gains.shape[1]), gains.shape
     )
@@ -1092,10 +1164,10 @@
         result[None],
         dx[None],
         enc_grad[None],
-        jnp.concatenate([o_qkv, o_qc, o_kvc], axis=1).reshape(qkv_weights.shape),
-        jnp.concatenate([o_o, o_oc], axis=1).reshape(out_weights.shape),
+        o_qkv.reshape(qkv_weights.shape),
+        o_out.reshape(out_weights.shape),
         o_in.reshape(ff_in.shape),
-        o_out,
+        o_down,
         s_gain,
         s_table,
     )

time: 235 us -> 234 us (level)
    unnamed x33 -> x23, local copies, waits for them, and re-layouts: 6.14 us -> 6.09 us
where the time goes in v3:
time: 234 us; the launch traced here: 233 us
  Pallas kernels  212 us (91%)
  local copies, waits for them, and re-layouts  18.9 us (8%)
    pallas_call x1, Pallas kernels, per_device(): pl.pallas_call(lambda *refs: layer_kernel(planes, tree, *[refs[i] for i i...  212 us
    unnamed x23, local copies, waits for them, and re-layouts  6.09 us

profile of v3, /device:TPU:0, one launch (start us, length us, event | category | flops | bytes accessed | tf_op | source)
XLA Modules:
  0.0 233.5 jit_solution(9495984538867326895)
XLA Ops:
  0.6 0.0 copy-start.2
  1.3 0.5 broadcast_in_dim.25.refs_3_
  1.9 0.7 slice.13
  2.6 0.1 rev.3
  2.7 1.2 add_bitcast_fusion.refs_0_
  3.9 1.5 dynamic_update_slice.4.refs_5_
  5.4 0.0 copy-start.7
  5.4 1.4 copy.24.refs_10_
  6.8 0.0 copy-done.7
  6.8 1.6 reshape_reshape.19.refs_7_
  8.4 0.0 copy-done.2
  8.4 0.8 reshape_reshape.20.refs_8_
  9.2 0.1 copy-done.1
  9.3 0.1 copy.23
  9.4 1.0 reshape_reshape.18.refs_6_
  10.3 212.0 %layer.1 = (bf16[64,768]{1,0:T(8,128)(2,1)}, bf16[128,768]{1,0:T(8,128)(2,1)}, f32[3,8,4608]{2,1,0:T(8,128)}, f32[3,8,1536]{2,1,0:T(8,128)}, f32[3,8,4096]{2,1,0...) custom-call(s32[1,128]{1,0:T(1,128)} %add_bitcast_fusion.refs_0_, ...), custom_call_target="tpu_custom_call" | custom-call | tf_op jit(solution)/shard_map/layer/pallas_call | solution.py:1144
  222.3 1.3 slice_bitcast_fusion
  223.6 0.7 slice.14
  224.3 0.6 constant_dynamic-slice_fusion
  225.0 1.7 reshape_reshape.22
  226.7 2.1 reshape_reshape.23
  228.8 0.1 reshape_reshape.21
  228.9 0.0 copy-start.5
  228.9 0.9 copy.25
  229.8 0.0 copy-done.5
  229.9 0.7 copy.32
  230.5 0.3 copy-done.4
  230.9 0.7 copy.33
  231.5 0.3 copy-done.6
  231.8 0.6 copy.34
  232.5 0.3 copy-done.3
  232.8 0.7 copy.35
  (7 shorter events, 0.0 us)
Async XLA Ops:
  0.6 7.7 %copy-start.2 = (bf16[24,2,2048]{2,1,0:T(2,128)(2,1)S(1)}, bf16[24,2,2048]{2,1,0:T(2,128)(2,1)}, u32[]{:S(2)}) copy-start(bf16[24,2,2048]{2,1,0:T(2,128)(2,1)} %param.17) | copy-start | bytes 589828
  5.4 1.4 copy-start.7
  8.4 0.9 copy-start.1
  226.7 2.1 copy-start
  228.9 0.9 copy-start.5
  229.9 1.0 copy-start.4
  230.9 1.0 copy-start.6
  231.8 1.0 copy-start.3
